TPU v7x, 32 devices: a whole 2x2x4 slice. The times are simulated.
32 devices in a mesh: dp: 4 (over y, x), row: 2 (over core), col: 4 (over z).
Axes of the slice: x: 2, y: 2, z: 4, core: 2. Of those that a mesh axis runs over, the one named last changes fastest.
Arguments:
- features: bfloat16 [4, 40, 160, 640], P('dp', 'row', 'col'), may hold values from -800 to 800
- hole_mask: int32 [4, 40, 160], P('dp', 'row', 'col'), may hold values 0 or 1
- norm_gain: float32 [640], replicated, may hold values from 0.5 to 1.5
- norm_shift: float32 [640], replicated, may hold values from -3 to 3
- conv_weight: bfloat16 [9, 640, 640], P(None, 'dp'), may hold values from -0.078125 to 0.078125
- mask_weight: float32 [9, 640], replicated, may hold values from -3 to 3
- conv_bias: float32 [640], replicated, may hold values from -3 to 3
Outputs:
- conv_out: bfloat16 [4, 40, 160, 640], P('dp', 'row', 'col')
All inputs are finite; a program needn't handle non-finite values. No bound on the sum of `hole_mask` on one device may be relied on, other than what follows from the above.
Results may differ from a plain program's by a relative error of at most 0.0032.
Values may be sent and summed in bfloat16 or wider, within the bound.
No kernel may reach another device: no remote copies, remote signals or barrier semaphores. Data moves between devices by JAX's collectives and lax.ppermute only.
A program may use at most 128 MiB of HBM per device.

v0:
```python
import jax
import jax.numpy as jnp
from jax import lax
from jax.sharding import PartitionSpec as P

GROUPS = 32


EPS = 1e-05


def with_halo(cells, sides, width):
    for axis, dim in sides:
        count = lax.axis_size(axis)
        ends = count - 1
        head = lax.slice_in_dim(cells, 0, width, axis=dim)
        tail = lax.slice_in_dim(cells, cells.shape[dim] - width, cells.shape[dim], axis=dim)
        cells = jnp.concatenate(
            [
                lax.ppermute(tail, axis, [(i, (i + 1) % count) for i in range(ends)]),
                cells,
                lax.ppermute(head, axis, [((i + 1) % count, i) for i in range(ends)]),
            ],
            axis=dim,
        )
    return cells


def local(features, hole_mask, norm_gain, norm_shift, conv_weight, mask_weight, conv_bias):
    rows_here = features.shape[1]
    cols_here = features.shape[2]
    channels = features.shape[3]
    cells = rows_here * cols_here
    count = cells * (channels // GROUPS) * lax.axis_size("row") * lax.axis_size("col")
    grouped = (
        features[0].astype(jnp.float32).reshape(rows_here, cols_here, GROUPS, channels // GROUPS)
    )
    sums = lax.psum(jnp.sum(grouped, axis=(0, 1, 3)), ("row", "col"))
    mean_val = sums / count
    deviate = grouped - mean_val[None, None, :, None]
    squares = lax.psum(jnp.sum(deviate * deviate, axis=(0, 1, 3)), ("row", "col"))
    var_val = squares / count
    normed = (deviate * lax.rsqrt(var_val + EPS)[None, None, :, None]).reshape(
        rows_here, cols_here, channels
    )
    act_low = jax.nn.silu(normed * norm_gain + norm_shift).astype(jnp.bfloat16)
    padded = with_halo(act_low, (("row", 0), ("col", 1)), 1)
    mask_low = hole_mask[0].astype(jnp.bfloat16)
    mask_pad = with_halo(mask_low, (("row", 0), ("col", 1)), 1).astype(jnp.float32)
    base_term = jnp.zeros((rows_here, cols_here, channels), jnp.float32) + conv_bias
    for tap in range(9):
        row_off = tap // 3
        col_off = tap % 3
        base_term = (
            base_term
            + mask_pad[row_off : row_off + rows_here, col_off : col_off + cols_here, None]
            * mask_weight[tap]
        )

    def window_of(tap):
        row_off = tap // 3
        col_off = tap % 3
        return padded[row_off : row_off + rows_here, col_off : col_off + cols_here]

    piece = lax.all_gather(conv_weight, "dp", axis=1, tiled=True)
    depth = piece.shape[1]
    stacked = jnp.concatenate([window_of(tap).reshape(cells, depth) for tap in range(9)], axis=1)
    total = jnp.dot(
        stacked, piece.reshape(9 * depth, piece.shape[2]), preferred_element_type=jnp.float32
    )
    conv_out = (total.reshape(rows_here, cols_here, channels) + base_term).astype(jnp.bfloat16)
    return conv_out[None]


def solution(mesh):
    in_specs = (
        P("dp", "row", "col", None),
        P("dp", "row", "col"),
        P(),
        P(),
        P(None, "dp", None),
        P(),
        P(),
    )
    out_specs = P("dp", "row", "col", None)
    return jax.shard_map(local, mesh=mesh, in_specs=in_specs, out_specs=out_specs, check_vma=False)
```

profile of v0, /device:TPU:0, one launch (start us, length us, event | category | flops | bytes accessed | tf_op | source)
XLA Modules:
  0.0 111.0 jit_solution(2881225508541470771)
XLA Ops:
  8.2 18.5 %psum.14 = f32[32]{0:T(128)S(1)} all-reduce(f32[32]{0:T(128)S(1)} %reduce_sum.25), channel_id=1, replica_groups=mesh['dp'=4,'row'=2,'col'=4] {'row','col'}, use_global_device_ids=true, to_apply=%region_2.0 | all-reduce | flops 32 | bytes 256 | tf_op jit(solution)/shard_map/psum | solution.py:38
  27.4 13.7 %psum.15 = f32[32]{0:T(128)S(1)} all-reduce(f32[32]{0:T(128)S(1)} %reduce_sum.37), channel_id=1, replica_groups=mesh['dp'=4,'row'=2,'col'=4] {'row','col'}, use_global_device_ids=true, to_apply=%region_5.6 | all-reduce | flops 32 | bytes 256 | tf_op jit(solution)/shard_map/psum | solution.py:41
  42.1 2.3 %collective-permute-start = (bf16[1,40,640]{2,1,0:T(8,128)(2,1)S(1)}, bf16[1,40,640]{2,1,0:T(8,128)(2,1)S(1)}, u32[]{:S(2)}, u32[]{:S(2)}) collective-permute-start(bf16[1,40,640]{2,1,0:T(8,128)(2,1)S(1)} %get-tuple-element.18), channel_id=1, source_target_pairs={{0,4},{1,5},{2,6},{3,7},{8,12},{9,13},{10,14},{11,15},{16,20},{17,... | collective-permute-start | bytes 153608 | tf_op jit(solution)/shard_map/ppermute | solution.py:20
  44.4 1.3 %collective-permute-start.1 = (bf16[1,40,640]{2,1,0:T(8,128)(2,1)S(1)}, bf16[1,40,640]{2,1,0:T(8,128)(2,1)S(1)}, u32[]{:S(2)}, u32[]{:S(2)}) collective-permute-start(bf16[1,40,640]{2,1,0:T(8,128)(2,1)S(1)} %get-tuple-element.19), channel_id=1, source_target_pairs={{4,0},{5,1},{6,2},{7,3},{12,8},{13,9},{14,10},{15,11},{20,16},{21,... | collective-permute-start | bytes 153608 | tf_op jit(solution)/shard_map/ppermute | solution.py:22
  45.8 3.0 %collective-permute-start.4 = (bf16[1,40]{1,0:T(2,128)(2,1)S(1)}, bf16[1,40]{1,0:T(2,128)(2,1)S(1)}, u32[]{:S(2)}, u32[]{:S(2)}) collective-permute-start(bf16[1,40]{1,0:T(2,128)(2,1)S(1)} %get-tuple-element.29), channel_id=1, source_target_pairs={{0,4},{1,5},{2,6},{3,7},{8,12},{9,13},{10,14},{11,15},{16,20},{17,... | collective-permute-start | bytes 248 | tf_op jit(solution)/shard_map/ppermute | solution.py:20
  48.8 1.3 %collective-permute-start.5 = (bf16[1,40]{1,0:T(2,128)(2,1)S(1)}, bf16[1,40]{1,0:T(2,128)(2,1)S(1)}, u32[]{:S(2)}, u32[]{:S(2)}) collective-permute-start(bf16[1,40]{1,0:T(2,128)(2,1)S(1)} %get-tuple-element.30), channel_id=1, source_target_pairs={{4,0},{5,1},{6,2},{7,3},{12,8},{13,9},{14,10},{15,11},{20,16},{21,... | collective-permute-start | bytes 248 | tf_op jit(solution)/shard_map/ppermute | solution.py:22
  50.2 1.6 %collective-permute-done.5 = bf16[1,40]{1,0:T(2,128)(2,1)S(1)} collective-permute-done((bf16[1,40]{1,0:T(2,128)(2,1)S(1)}, bf16[1,40]{1,0:T(2,128)(2,1)S(1)}, u32[]{:S(2)}, u32[]{:S(2)}) %collective-permute-start.5) | collective-permute-done | bytes 112 | tf_op jit(solution)/shard_map/ppermute | solution.py:22
  51.9 3.7 %collective-permute-start.6 = (bf16[22,1]{1,0:T(8,128)(2,1)S(1)}, bf16[22,1]{1,0:T(8,128)(2,1)S(1)}, u32[]{:S(2)}, u32[]{:S(2)}) collective-permute-start(bf16[22,1]{1,0:T(8,128)(2,1)S(1)} %get-tuple-element.31), channel_id=1, source_target_pairs={{0,1},{1,2},{2,3},{4,5},{5,6},{6,7},{8,9},{9,10},{10,11},{12,13},{... | collective-permute-start | bytes 140 | tf_op jit(solution)/shard_map/ppermute | solution.py:20
  55.6 1.3 %collective-permute-start.7 = (bf16[22,1]{1,0:T(8,128)(2,1)S(1)}, bf16[22,1]{1,0:T(8,128)(2,1)S(1)}, u32[]{:S(2)}, u32[]{:S(2)}) collective-permute-start(bf16[22,1]{1,0:T(8,128)(2,1)S(1)} %get-tuple-element.32), channel_id=1, source_target_pairs={{1,0},{2,1},{3,2},{5,4},{6,5},{7,6},{9,8},{10,9},{11,10},{13,12},{... | collective-permute-start | bytes 140 | tf_op jit(solution)/shard_map/ppermute | solution.py:22
  56.9 4.2 %collective-permute-done.7 = bf16[22,1]{1,0:T(8,128)(2,1)S(1)} collective-permute-done((bf16[22,1]{1,0:T(8,128)(2,1)S(1)}, bf16[22,1]{1,0:T(8,128)(2,1)S(1)}, u32[]{:S(2)}, u32[]{:S(2)}) %collective-permute-start.7) | collective-permute-done | bytes 76 | tf_op jit(solution)/shard_map/ppermute | solution.py:22
  61.3 1.9 %collective-permute-start.2 = (bf16[22,1,640]{2,1,0:T(2,128)(2,1)S(1)}, bf16[22,1,640]{2,1,0:T(2,128)(2,1)S(1)}, u32[]{:S(2)}, u32[]{:S(2)}) collective-permute-start(bf16[22,1,640]{2,1,0:T(2,128)(2,1)S(1)} %get-tuple-element.17), channel_id=1, source_target_pairs={{0,1},{1,2},{2,3},{4,5},{5,6},{6,7},{8,9},{9,10},{10,11},{12,13},{... | collective-permute-start | bytes 84488 | tf_op jit(solution)/shard_map/ppermute | solution.py:20
  63.2 1.3 %collective-permute-start.3 = (bf16[22,1,640]{2,1,0:T(2,128)(2,1)S(1)}, bf16[22,1,640]{2,1,0:T(2,128)(2,1)S(1)}, u32[]{:S(2)}, u32[]{:S(2)}) collective-permute-start(bf16[22,1,640]{2,1,0:T(2,128)(2,1)S(1)} %get-tuple-element.16), channel_id=1, source_target_pairs={{1,0},{2,1},{3,2},{5,4},{6,5},{7,6},{9,8},{10,9},{11,10},{13,12},{... | collective-permute-start | bytes 84488 | tf_op jit(solution)/shard_map/ppermute | solution.py:22
  65.0 4.3 %collective-permute-done.3 = bf16[22,1,640]{2,1,0:T(2,128)(2,1)S(1)} collective-permute-done((bf16[22,1,640]{2,1,0:T(2,128)(2,1)S(1)}, bf16[22,1,640]{2,1,0:T(2,128)(2,1)S(1)}, u32[]{:S(2)}, u32[]{:S(2)}) %collective-permute-start.3) | collective-permute-done | bytes 28192 | tf_op jit(solution)/shard_map/ppermute | solution.py:22
  70.1 1.1 %slice_dynamic-update-slice_fusion.5 = bf16[20,40,5760]{2,1,0:T(8,128)(2,1)} fusion(bf16[22,41,640]{2,1,0:T(8,128)(2,1)S(1)} %get-tuple-element.15), kind=kLoop, calls=%fused_computation.28 | loop fusion | bytes 2048000
  71.2 1.2 %fusion.14 = bf16[20,40,5760]{2,1,0:T(8,128)(2,1)} fusion(bf16[20,40,5760]{2,1,0:T(8,128)(2,1)} %slice_dynamic-update-slice_fusion.5, bf16[20,40,640]{2,1,0:T(8,128)(2,1)S(1)} %fusion.9, bf16[1,40,640]{2,1,0:T(8,128)(2,1)S(1)} %collective-permute-done), kind=kLoop, calls=%fused_computation.27 | loop fusion | flops 2048000 | bytes 2099200
  72.4 1.3 %slice_dynamic-update-slice_fusion.4 = bf16[20,40,5760]{2,1,0:T(8,128)(2,1)} fusion(bf16[20,40,5760]{2,1,0:T(8,128)(2,1)} %fusion.14, bf16[22,41,640]{2,1,0:T(8,128)(2,1)S(1)} %get-tuple-element.14), kind=kLoop, calls=%fused_computation.25 | loop fusion | bytes 2048000
  73.7 1.1 %slice_dynamic-update-slice_fusion.3 = bf16[20,40,5760]{2,1,0:T(8,128)(2,1)} fusion(bf16[20,40,5760]{2,1,0:T(8,128)(2,1)} %slice_dynamic-update-slice_fusion.4, bf16[22,41,640]{2,1,0:T(8,128)(2,1)S(1)} %get-tuple-element.15), kind=kLoop, calls=%fused_computation.24 | loop fusion | bytes 2048000
  74.9 1.7 %constant_dynamic-update-slice_fusion = bf16[20,40,5760]{2,1,0:T(8,128)(2,1)} fusion(bf16[20,40,5760]{2,1,0:T(8,128)(2,1)} %slice_dynamic-update-slice_fusion.3, f32[640]{0:T(1024)S(1)} %copy-done.1, f32[640]{0:T(1024)S(1)} %copy-done.2, f32[640]{0:T(1024)S(1)} %mul.172, f32[640]{0:T(1024)S(1)} %sub.21, bf16[1,20,40,640]{3,2,1,0:T(8,128)(2,1)S(1)} %copy-done), kind=kLoop, calls=%fused_computation.32 | loop fusion | flops 5120000 | bytes 2058240
  76.6 1.4 %slice_dynamic-update-slice_fusion.2 = bf16[20,40,5760]{2,1,0:T(8,128)(2,1)} fusion(bf16[20,40,5760]{2,1,0:T(8,128)(2,1)} %constant_dynamic-update-slice_fusion, bf16[22,41,640]{2,1,0:T(8,128)(2,1)S(1)} %get-tuple-element.14), kind=kLoop, calls=%fused_computation.23 | loop fusion | bytes 2048000
  78.0 1.1 slice_dynamic-update-slice_fusion.1
  79.1 1.1 %fusion.13 = bf16[20,40,5760]{2,1,0:T(8,128)(2,1)} fusion(bf16[20,40,5760]{2,1,0:T(8,128)(2,1)} %slice_dynamic-update-slice_fusion.1, bf16[1,40,640]{2,1,0:T(8,128)(2,1)S(1)} %collective-permute-done.1, bf16[20,40,640]{2,1,0:T(8,128)(2,1)S(1)} %fusion.9), kind=kLoop, calls=%fused_computation.21 | loop fusion | flops 2048000 | bytes 2099200
  80.2 1.4 %slice_dynamic-update-slice_fusion = bf16[20,40,5760]{2,1,0:T(8,128)(2,1)} fusion(bf16[20,40,5760]{2,1,0:T(8,128)(2,1)} %fusion.13, bf16[22,41,640]{2,1,0:T(8,128)(2,1)S(1)} %get-tuple-element.14), kind=kLoop, calls=%fused_computation.19 | loop fusion | bytes 2048000 | tf_op jit(solution)/shard_map/concatenate | solution.py:67
  81.5 9.4 %all-gather.2.cloned.1.call-done = bf16[9,640,640]{2,1,0:T(8,128)(2,1)} async-done(((bf16[9,160,640]{2,1,0:T(8,128)(2,1)}), bf16[9,640,640]{2,1,0:T(8,128)(2,1)}) %all-gather.2.cloned.1.call-update) | async-done | bytes 7372816 | tf_op jit(solution)/shard_map/all_gather | solution.py:65
  91.0 13.2 %fusion.12 = bf16[1,20,40,640]{3,2,1,0:T(8,128)(2,1)} fusion(bf16[20,40,5760]{2,1,0:T(8,128)(2,1)} %slice_dynamic-update-slice_fusion, bf16[5760,640,1]{1,0,2:T(8,128)(2,1)} %bitcast.42, f32[640]{0:T(1024)S(1)} %get-tuple-element.12, f32[20,40]{1,0:T(8,128)S(1)} %get-tuple-element.21, f32[640]{0:T(1024)S(1)} %get-tuple-element.13, ...), kind=kOutput, calls=%fused_computation.16 | convolution fusion | flops 5908480000 | bytes 17667200 | tf_op jit(solution)/shard_map/dot_general | solution.py:68
  (43 shorter events, 4.9 us)
Async XLA Ops:
  6.5 1.2 %copy-start = (bf16[1,20,40,640]{3,2,1,0:T(8,128)(2,1)S(1)}, bf16[1,20,40,640]{3,2,1,0:T(8,128)(2,1)}, u32[]{:S(2)}) copy-start(bf16[1,20,40,640]{3,2,1,0:T(8,128)(2,1)} %param.7) | copy-start | bytes 3072004
  6.5 34.8 %copy-start.1 = (f32[640]{0:T(1024)S(1)}, f32[640]{0:T(1024)}, u32[]{:S(2)}) copy-start(f32[640]{0:T(1024)} %param.10) | copy-start | bytes 7684
  6.5 34.8 %copy-start.2 = (f32[640]{0:T(1024)S(1)}, f32[640]{0:T(1024)}, u32[]{:S(2)}) copy-start(f32[640]{0:T(1024)} %param.9) | copy-start | bytes 7684
  6.5 84.4 %all-gather.2.cloned.1.call-start = ((), (), s32[]{:S(2)}) async-start(), calls=%async_computation | async-start | bytes 9216000 | tf_op jit(solution)/shard_map/all_gather | solution.py:65
  7.8 38.0 %copy-start.4 = (s32[1,20,40]{2,0,1:T(1,128)S(1)}, s32[1,20,40]{2,0,1:T(1,128)}, u32[]{:S(2)}) copy-start(s32[1,20,40]{2,0,1:T(1,128)} %param.8) | copy-start | bytes 9604
  7.8 42.3 %copy-start.3 = (f32[9,640]{1,0:T(8,128)S(1)}, f32[9,640]{1,0:T(8,128)}, u32[]{:S(2)}) copy-start(f32[9,640]{1,0:T(8,128)} %param.12) | copy-start | bytes 69124
  42.1 19.1 %collective-permute-start = (bf16[1,40,640]{2,1,0:T(8,128)(2,1)S(1)}, bf16[1,40,640]{2,1,0:T(8,128)(2,1)S(1)}, u32[]{:S(2)}, u32[]{:S(2)}) collective-permute-start(bf16[1,40,640]{2,1,0:T(8,128)(2,1)S(1)} %get-tuple-element.18), channel_id=1, source_target_pairs={{0,4},{1,5},{2,6},{3,7},{8,12},{9,13},{10,14},{11,15},{16,20},{17,... | collective-permute-start | bytes 153608 | tf_op jit(solution)/shard_map/ppermute | solution.py:20
  44.4 16.8 %collective-permute-start.1 = (bf16[1,40,640]{2,1,0:T(8,128)(2,1)S(1)}, bf16[1,40,640]{2,1,0:T(8,128)(2,1)S(1)}, u32[]{:S(2)}, u32[]{:S(2)}) collective-permute-start(bf16[1,40,640]{2,1,0:T(8,128)(2,1)S(1)} %get-tuple-element.19), channel_id=1, source_target_pairs={{4,0},{5,1},{6,2},{7,3},{12,8},{13,9},{14,10},{15,11},{20,16},{21,... | collective-permute-start | bytes 153608 | tf_op jit(solution)/shard_map/ppermute | solution.py:22
  45.8 4.4 %collective-permute-start.4 = (bf16[1,40]{1,0:T(2,128)(2,1)S(1)}, bf16[1,40]{1,0:T(2,128)(2,1)S(1)}, u32[]{:S(2)}, u32[]{:S(2)}) collective-permute-start(bf16[1,40]{1,0:T(2,128)(2,1)S(1)} %get-tuple-element.29), channel_id=1, source_target_pairs={{0,4},{1,5},{2,6},{3,7},{8,12},{9,13},{10,14},{11,15},{16,20},{17,... | collective-permute-start | bytes 248 | tf_op jit(solution)/shard_map/ppermute | solution.py:20
  48.8 3.1 %collective-permute-start.5 = (bf16[1,40]{1,0:T(2,128)(2,1)S(1)}, bf16[1,40]{1,0:T(2,128)(2,1)S(1)}, u32[]{:S(2)}, u32[]{:S(2)}) collective-permute-start(bf16[1,40]{1,0:T(2,128)(2,1)S(1)} %get-tuple-element.30), channel_id=1, source_target_pairs={{4,0},{5,1},{6,2},{7,3},{12,8},{13,9},{14,10},{15,11},{20,16},{21,... | collective-permute-start | bytes 248 | tf_op jit(solution)/shard_map/ppermute | solution.py:22
  51.9 5.0 %collective-permute-start.6 = (bf16[22,1]{1,0:T(8,128)(2,1)S(1)}, bf16[22,1]{1,0:T(8,128)(2,1)S(1)}, u32[]{:S(2)}, u32[]{:S(2)}) collective-permute-start(bf16[22,1]{1,0:T(8,128)(2,1)S(1)} %get-tuple-element.31), channel_id=1, source_target_pairs={{0,1},{1,2},{2,3},{4,5},{5,6},{6,7},{8,9},{9,10},{10,11},{12,13},{... | collective-permute-start | bytes 140 | tf_op jit(solution)/shard_map/ppermute | solution.py:20
  55.6 5.5 %collective-permute-start.7 = (bf16[22,1]{1,0:T(8,128)(2,1)S(1)}, bf16[22,1]{1,0:T(8,128)(2,1)S(1)}, u32[]{:S(2)}, u32[]{:S(2)}) collective-permute-start(bf16[22,1]{1,0:T(8,128)(2,1)S(1)} %get-tuple-element.32), channel_id=1, source_target_pairs={{1,0},{2,1},{3,2},{5,4},{6,5},{7,6},{9,8},{10,9},{11,10},{13,12},{... | collective-permute-start | bytes 140 | tf_op jit(solution)/shard_map/ppermute | solution.py:22
  61.3 3.7 %collective-permute-start.2 = (bf16[22,1,640]{2,1,0:T(2,128)(2,1)S(1)}, bf16[22,1,640]{2,1,0:T(2,128)(2,1)S(1)}, u32[]{:S(2)}, u32[]{:S(2)}) collective-permute-start(bf16[22,1,640]{2,1,0:T(2,128)(2,1)S(1)} %get-tuple-element.17), channel_id=1, source_target_pairs={{0,1},{1,2},{2,3},{4,5},{5,6},{6,7},{8,9},{9,10},{10,11},{12,13},{... | collective-permute-start | bytes 84488 | tf_op jit(solution)/shard_map/ppermute | solution.py:20
  63.2 6.1 %collective-permute-start.3 = (bf16[22,1,640]{2,1,0:T(2,128)(2,1)S(1)}, bf16[22,1,640]{2,1,0:T(2,128)(2,1)S(1)}, u32[]{:S(2)}, u32[]{:S(2)}) collective-permute-start(bf16[22,1,640]{2,1,0:T(2,128)(2,1)S(1)} %get-tuple-element.16), channel_id=1, source_target_pairs={{1,0},{2,1},{3,2},{5,4},{6,5},{7,6},{9,8},{10,9},{11,10},{13,12},{... | collective-permute-start | bytes 84488 | tf_op jit(solution)/shard_map/ppermute | solution.py:22
  79.1 11.9 %copy-start.5 = (f32[640]{0:T(1024)S(1)}, f32[640]{0:T(1024)}, u32[]{:S(2)}) copy-start(f32[640]{0:T(1024)} %param.13) | copy-start | bytes 7684
Sparse Core Ops, SparseCore 0:
  9.2 81.7 all-gather.1
where the time goes:
time: 111 us
  blocking collectives  32.3 us (29%)
  waiting for transfers between devices  20.7 us (19%)
  starting transfers between devices  16.1 us (15%)
  between operations  13.6 us (12%)
  matrix products  13.2 us (12%)
  local copies, waits for them, and re-layouts  8.69 us (8%)
  other arithmetic  6.5 us (6%)
    psum x1, blocking collectives, local(): sums = lax.psum(jnp.sum(grouped, axis=(0, 1, 3)), ('row', 'col'))  18.5 us
    psum x1, blocking collectives, local(): lax.psum(jnp.sum(deviate * deviate, axis=(0, 1, 3)), ('row', 'col'))  13.7 us
    dot_general x1, matrix products, local(): jnp.dot(stacked, piece.reshape(9 * depth, piece.shape[2]), preferred_elem...  13.2 us
    ppermute x4, starting transfers between devices, with_halo(): lax.ppermute(tail, axis, [(i, (i + 1) % count) for i in range(ends)])  10.9 us
    ppermute x4, waiting for transfers between devices, with_halo(): lax.ppermute(head, axis, [((i + 1) % count, i) for i in range(ends)])  10.1 us
    all_gather x1, waiting for transfers between devices, local(): piece = lax.all_gather(conv_weight, 'dp', axis=1, tiled=True)  9.41 us
    unnamed x18, local copies, waits for them, and re-layouts  6.54 us
    ppermute x4, starting transfers between devices, with_halo(): lax.ppermute(head, axis, [((i + 1) % count, i) for i in range(ends)])  5.17 us
  transfers between devices with their start and end apart: 9, of which 5 were waited for; matrix products, arithmetic and copies ran while one was open for 13% of the time, Pallas kernels for 0%

commit v1 on v0

v1 whole, which is shorter than its diff:
```python
import functools

import jax
import jax.numpy as jnp
from jax import lax
from jax.experimental import pallas as pl
from jax.experimental.pallas import tpu as pltpu
from jax.sharding import PartitionSpec as P


GROUPS = 32
EPS = 1e-05
TAPS = 9
PARTS = 4
LANES = 128


VMEM = pl.BlockSpec(memory_space=pltpu.VMEM)
HBM = pl.BlockSpec(memory_space=pltpu.HBM)
F32 = jnp.float32
BF16 = jnp.bfloat16


def swap(value, axis, bit):
    size = lax.axis_size(axis)
    return lax.ppermute(value, axis, [(i, i ^ bit) for i in range(size)])


def shift(value, axis, step):
    size = lax.axis_size(axis)
    pairs = [(i, i + step) for i in range(size) if 0 <= i + step < size]
    return lax.ppermute(value, axis, pairs)


def after(value, *others):
    return lax.optimization_barrier((value, *others))[0]


def params(mib):
    return pltpu.CompilerParams(vmem_limit_bytes=mib << 20)


def cost(flops, size):
    return pl.CostEstimate(flops=flops, bytes_accessed=size, transcendentals=0)


def thirds(value):
    high = value.astype(BF16)
    rest = value - high.astype(F32)
    middle = rest.astype(BF16)
    low = (rest - middle.astype(F32)).astype(BF16)
    return high, middle, low


def exact_dot(value, ones, dims):
    total = None
    for piece in thirds(value):
        term = lax.dot_general(piece, ones, (dims, ((), ())), preferred_element_type=F32)
        total = term if total is None else total + term
    return total


def by_group(value, member):
    return exact_dot(jnp.broadcast_to(value, (16, value.shape[1])), member, ((1,), (0,)))[:1]


def by_channel(value, member):
    return exact_dot(jnp.broadcast_to(value, (16, value.shape[1])), member, ((1,), (1,)))[:1]


def merged(mean, spread, other_mean, other_spread, count):
    gap = mean - other_mean
    return (mean + other_mean) * 0.5, spread + other_spread + gap * gap * (count * 0.5)


def edges_kept(count_row, count_col):
    row, col = lax.axis_index("row"), lax.axis_index("col")
    inside = (row > 0, row < count_row - 1, col > 0, col < count_col - 1)
    return [jnp.where(flag, 1.0, 0.0).astype(F32) for flag in inside]


def even_col():
    return lax.rem(lax.axis_index("col"), 2) == 0


def segments(half, depth, rows):
    pieces = []
    at = half * rows
    while at < (half + 1) * rows:
        tap, first = divmod(at, depth)
        width = min(depth - first, (half + 1) * rows - at)
        pieces.append((tap, first, width))
        at += width
    return pieces


def cut_kernel(weight, head, tail, sems):
    rows, first = head.shape[0] + tail.shape[0], head.shape[0]
    at = pl.multiple_of(lax.rem(lax.axis_index("row"), 2) * rows, 16)
    one = pltpu.make_async_copy(weight.at[pl.ds(at, first)], head, sems.at[0])
    two = pltpu.make_async_copy(
        weight.at[pl.ds(pl.multiple_of(at + first, 16), rows - first)], tail, sems.at[1]
    )
    one.start()
    two.start()
    one.wait()
    two.wait()


def stats_kernel(per_group, cells, mask, member, up, down, stats):
    rows, cols, channels = cells.shape
    count = float(rows * cols)
    total = jnp.zeros((cols, channels), F32)
    for r in range(rows):
        total = total + cells[r].astype(F32)
    sums = jnp.sum(total, axis=0, keepdims=True)
    mean = by_group(sums, member[...]) * (1.0 / (count * per_group))
    wide = by_channel(mean, member[...])
    total = jnp.zeros((cols, channels), F32)
    for r in range(rows):
        away = cells[r].astype(F32) - wide
        total = total + away * away
    spread = by_group(jnp.sum(total, axis=0, keepdims=True), member[...])
    lines = lax.broadcasted_iota(jnp.int32, (8, LANES), 0)
    block = jnp.where(lines == 0, mean, jnp.where(lines == 1, spread, 0.0))
    stats[...] = block
    for out, r in ((up, 0), (down, rows - 1)):
        out[:cols, :] = cells[r].astype(F32)
        out[cols:, :] = jnp.zeros((8, channels), F32)
        out[cols : cols + 8, :LANES] = block
        out[cols + 2 : cols + 3, :cols] = mask[r].astype(F32)


def first_message_kernel(count, sizes, cells, mask, above, below, own, other, near, far, stats):
    rows, cols, channels = cells.shape
    base = stats_row(rows)
    keep = edges_kept(*sizes)
    mean, spread = merged(own[0:1], own[1:2], other[0:1], other[1:2], count)
    lines = lax.broadcasted_iota(jnp.int32, (8, LANES), 0)
    block = jnp.where(lines == 0, mean, jnp.where(lines == 1, spread, 0.0))
    stats[...] = block
    lane = lax.broadcasted_iota(jnp.int32, (rows + 2, LANES), 1)
    edges = []
    for c in (0, cols - 1):
        body = jnp.concatenate(
            [above[c : c + 1, :], cells[:, c, :].astype(F32), below[c : c + 1, :]], axis=0
        )
        holes = jnp.concatenate(
            [
                above[cols + 2 : cols + 3, c : c + 1] * keep[0],
                mask[:, 0, :].astype(F32)[:, c : c + 1],
                below[cols + 2 : cols + 3, c : c + 1] * keep[1],
            ],
            axis=0,
        )
        edges.append((body, jnp.where(lane == 0, jnp.broadcast_to(holes, lane.shape), 0.0)))
    even = even_col()
    for out, swapped in ((near, False), (far, True)):
        first, last = edges[0], edges[1]
        if swapped:
            first, last = last, first
        out[...] = jnp.zeros(out.shape, BF16)
        out[: rows + 2, :channels] = jnp.where(even, last[0], first[0]).astype(BF16)
        out[: rows + 2, channels:] = jnp.where(even, last[1], first[1]).astype(BF16)
    near[base : base + 8, :LANES] = packed(mean, spread)


def stats_row(rows):
    return -(-(rows + 2) // 16) * 16


def packed(mean, spread):
    return jnp.concatenate(
        [*thirds(mean), *thirds(spread), jnp.zeros((2, mean.shape[1]), BF16)], axis=0
    )


def unpacked(message, base):
    block = message[base : base + 16, :LANES].astype(F32)
    return block[0:1] + block[1:2] + block[2:3], block[3:4] + block[4:5] + block[5:6]


def second_message_kernel(rows, count, far, own, got, out, stats):
    base = stats_row(rows)
    mean, spread = merged(own[0:1], own[1:2], *unpacked(got, base), count)
    lines = lax.broadcasted_iota(jnp.int32, (8, LANES), 0)
    stats[...] = jnp.where(lines == 0, mean, jnp.where(lines == 1, spread, 0.0))
    out[...] = far[...]
    out[base : base + 8, :LANES] = packed(mean, spread)


def windows_kernel(
    count, depth, half_rows, sizes, stride, cells, mask, above, below, near, far, own, member,
    norm_gain, norm_shift, mask_weight, bias, weight, out, total, even, odd, kept, holes,
):
    rows, cols, channels = cells.shape
    base = stats_row(rows)
    group = 2 * cols
    mean, spread = merged(own[0:1], own[1:2], *unpacked(far, base), count)
    mean_row = by_channel(mean, member[...])
    gain_row = by_channel(lax.rsqrt(spread * (0.5 / count) + EPS), member[...]) * norm_gain[...]
    offset_row = norm_shift[...]

    def act(x):
        v = (x.astype(F32) - mean_row) * gain_row + offset_row
        return v / (1.0 + jnp.exp(-v))

    keep = edges_kept(*sizes)
    is_even = even_col()
    from_near = near[: rows + 2, :].astype(F32)
    from_far = far[: rows + 2, :].astype(F32)
    left = jnp.where(is_even, from_far, from_near)
    right = jnp.where(is_even, from_near, from_far)
    left_act = act(left[:, :channels]) * keep[2]
    right_act = act(right[:, :channels]) * keep[3]
    place = lax.broadcasted_iota(jnp.int32, (cols, channels), 0)

    tall = jnp.concatenate(
        [
            above[cols + 2 : cols + 3, :cols] * keep[0],
            mask[:, 0, :].astype(F32),
            below[cols + 2 : cols + 3, :cols] * keep[1],
        ],
        axis=0,
    )
    tall = jnp.concatenate(
        [
            left[:, channels : channels + 1] * keep[2],
            tall,
            right[:, channels : channels + 1] * keep[3],
            jnp.zeros((rows + 2, LANES - cols - 2), F32),
        ],
        axis=1,
    )
    tall = jnp.concatenate([tall, jnp.zeros((LANES - rows - 2, LANES), F32)], axis=0)
    flipped = tall.T
    moved = [flipped[dx : dx + cols, :] for dx in range(3)]
    ending = jnp.concatenate([jnp.ones((cols, 1), F32), jnp.zeros((cols, 6), F32)], axis=1)

    def hole_row(r):
        return jnp.concatenate([m[:, r : r + 3] for m in moved] + [ending], axis=1)

    def row_of(r):
        if r == 0:
            value = act(above[:cols, :])
        elif r == rows + 1:
            value = act(below[:cols, :])
        else:
            value = act(cells[r - 1])
        lo, hi = left_act[r : r + 1], right_act[r : r + 1]
        if r == 0 or r == rows + 1:
            edge = keep[0] if r == 0 else keep[1]
            value, lo, hi = value * edge, lo * edge, hi * edge
        before = jnp.where(place == 0, jnp.broadcast_to(lo, value.shape), pltpu.roll(value, 1, 0))
        behind = jnp.where(
            place == cols - 1, jnp.broadcast_to(hi, value.shape), pltpu.roll(value, cols - 1, 0)
        )
        return before, value, behind

    for pair in range(rows // 2 + 1):
        one = row_of(2 * pair)
        two = row_of(2 * pair + 1)
        for dx in range(3):
            even[dx, pair * group : (pair + 1) * group, :] = jnp.concatenate(
                [one[dx], two[dx]], axis=0
            ).astype(BF16)
            if pair:
                odd[dx, (pair - 1) * group : pair * group, :] = jnp.concatenate(
                    [kept[dx], one[dx]], axis=0
                ).astype(BF16)
            kept[dx] = two[dx]
        if pair < rows // 2:
            holes[pair * group : (pair + 1) * group, :16] = jnp.concatenate(
                [hole_row(2 * pair), hole_row(2 * pair + 1)], axis=0
            ).astype(BF16)

    def fill(step, carry):
        at = pl.multiple_of(step * group, group)
        for part in range(PARTS):
            for half in range(2):
                pieces = []
                for tap, first, width in segments(half, depth, half_rows):
                    source = odd if tap // 3 == 1 else even
                    start = at + (group if tap // 3 == 2 else 0)
                    lane = part * depth + first
                    pieces.append(source[tap % 3, pl.ds(start, group), lane : lane + width])
                out[2 * part + half, pl.ds(at, group), :] = jnp.concatenate(pieces, axis=1)
        return carry

    lax.fori_loop(0, rows // 2, fill, 0)

    taps = mask_weight[...]
    order = [3 * (k % 3) + k // 3 for k in range(TAPS)]
    table = jnp.concatenate(
        [taps[t : t + 1] for t in order] + [bias[...], jnp.zeros((6, channels), F32)], axis=0
    )
    part = lax.axis_index("dp") // stride
    spots = 2 * part, 2 * part + 1
    result = None
    for piece in thirds(table):
        term = jnp.dot(holes[:, :16], piece, preferred_element_type=F32)
        result = term if result is None else result + term
    for half in range(2):
        result = result + jnp.dot(
            out[spots[half]],
            weight[half * half_rows : (half + 1) * half_rows, :],
            preferred_element_type=F32,
        )
    total[...] = result


def next_kernel(stride, flip, lhs, one, two, three, four, total, out, held):
    cut = one.shape[0]
    owner = (lax.axis_index("dp") // stride) ^ flip
    core = lax.rem(lax.axis_index("row"), 2)
    spots = 2 * owner + core, 2 * owner + 1 - core
    for spot, (head, tail) in enumerate(((one, two), (three, four))):
        held[spot, :cut, :] = head[...]
        held[spot, cut:, :] = tail[...]
    out[...] = (
        total[...]
        + jnp.dot(lhs[spots[0]], held[0], preferred_element_type=F32)
        + jnp.dot(lhs[spots[1]], held[1], preferred_element_type=F32)
    ).astype(out.dtype)


def local(features, hole_mask, norm_gain, norm_shift, conv_weight, mask_weight, conv_bias):
    rows, cols, channels = features.shape[1:]
    cells = rows * cols
    per_group = channels // GROUPS
    n_dp, n_row, n_col = lax.axis_size("dp"), lax.axis_size("row"), lax.axis_size("col")
    if n_col != 4 or rows % 2 or cols % 8:
        raise ValueError("unsupported sizes")
    stride = n_dp // PARTS
    at_dp, at_row = lax.axis_index("dp"), lax.axis_index("row")

    shard = conv_weight
    bit = 1
    while bit < stride:
        other = swap(shard, "dp", bit)
        upper = (at_dp // bit) % 2 == 1
        shard = jnp.concatenate(
            [jnp.where(upper, other, shard), jnp.where(upper, shard, other)], axis=1
        )
        bit *= 2
    depth = shard.shape[1]
    weight = shard.reshape(TAPS * depth, channels)
    half_rows = TAPS * depth // 2
    first = -(-(half_rows // 2) // LANES) * LANES

    piece_a, piece_b = pl.pallas_call(
        cut_kernel,
        out_shape=[
            jax.ShapeDtypeStruct((first, channels), BF16),
            jax.ShapeDtypeStruct((half_rows - first, channels), BF16),
        ],
        in_specs=[HBM],
        out_specs=[VMEM, VMEM],
        scratch_shapes=[pltpu.SemaphoreType.DMA((2,))],
        compiler_params=params(4),
        name="cut",
    )(pltpu.with_memory_space_constraint(weight, pltpu.HBM))
    x_b = swap(piece_b, "dp", stride)
    y_a = swap(piece_a, "dp", 2 * stride)

    image = features[0]
    mask = hole_mask.reshape(rows, 1, cols)
    member = (
        lax.broadcasted_iota(jnp.int32, (channels, LANES), 0) // per_group
        == lax.broadcasted_iota(jnp.int32, (channels, LANES), 1)
    ).astype(BF16)
    stats_shape = jax.ShapeDtypeStruct((8, LANES), F32)
    line_shape = jax.ShapeDtypeStruct((cols + 8, channels), F32)
    up, down, stats = pl.pallas_call(
        functools.partial(stats_kernel, per_group),
        out_shape=[line_shape, line_shape, stats_shape],
        in_specs=[VMEM] * 3,
        out_specs=[VMEM] * 3,
        compiler_params=params(4),
        cost_estimate=cost(0, 4 << 20),
        name="stats",
    )(image, mask, member)
    x_a = swap(after(piece_a, stats), "dp", stride)
    y_b = swap(after(piece_b, stats), "dp", 2 * stride)
    count = float(cells * per_group)
    if n_row == 2:
        above = below = swap(jnp.where(at_row == 0, down, up), "row", 1)
        other = above[cols : cols + 8, :LANES]
    else:
        above = shift(down, "row", 1)
        below = shift(up, "row", -1)
        bit = 1
        other = swap(stats, "row", bit)
        while 2 * bit < n_row:
            mean, spread = merged(stats[0], stats[1], other[0], other[1], count)
            stats = jnp.concatenate([mean[None], spread[None], jnp.zeros((6, LANES), F32)])
            count *= 2.0
            bit *= 2
            other = swap(stats, "row", bit)

    message = jax.ShapeDtypeStruct((stats_row(rows) + 16, channels + LANES), BF16)
    near, far, stats = pl.pallas_call(
        functools.partial(first_message_kernel, count, (n_row, n_col)),
        out_shape=[message, message, stats_shape],
        in_specs=[VMEM] * 6,
        out_specs=[VMEM] * 3,
        compiler_params=params(4),
        cost_estimate=cost(0, 1 << 20),
        name="message_one",
    )(image, mask, above, below, stats, other)
    near = swap(near, "col", 1)
    count *= 2.0
    far, stats = pl.pallas_call(
        functools.partial(second_message_kernel, rows, count),
        out_shape=[message, stats_shape],
        in_specs=[VMEM] * 3,
        out_specs=[VMEM] * 2,
        compiler_params=params(4),
        cost_estimate=cost(0, 1 << 18),
        name="message_two",
    )(far, stats, near)
    far = swap(far, "col", 3)
    x_b, y_a = after(x_b, far), after(y_a, far)
    count *= 2.0
    d_a = swap(y_a, "dp", stride)
    d_b = swap(x_b, "dp", 2 * stride)

    flops = 4 * cells * half_rows * channels
    lhs, total = pl.pallas_call(
        functools.partial(windows_kernel, count, depth, half_rows, (n_row, n_col), stride),
        out_shape=[
            pltpu.VMEM((2 * PARTS, cells, half_rows), BF16),
            pltpu.VMEM((cells, channels), F32),
        ],
        in_specs=[VMEM] * 13,
        out_specs=[VMEM, VMEM],
        scratch_shapes=[
            pltpu.VMEM((3, cells + 2 * cols, channels), BF16),
            pltpu.VMEM((3, cells, channels), BF16),
            pltpu.VMEM((3, cols, channels), F32),
            pltpu.VMEM((cells, LANES), BF16),
        ],
        compiler_params=params(14),
        cost_estimate=cost(2 * flops, 24 << 20),
        name="windows",
    )(
        image, mask, above, below, near, far, stats, member,
        norm_gain[None], norm_shift[None], mask_weight, conv_bias[None], weight,
    )

    x_a, y_b = after(x_a, lhs), after(y_b, lhs)
    for number, (head, tail) in enumerate(((x_a, x_b), (y_a, y_b), (d_a, d_b))):
        last = number == 2
        total = pl.pallas_call(
            functools.partial(next_kernel, stride, number + 1),
            out_shape=jax.ShapeDtypeStruct((cells, channels), BF16)
            if last
            else pltpu.VMEM((cells, channels), F32),
            in_specs=[VMEM] * 6,
            out_specs=VMEM,
            scratch_shapes=[pltpu.VMEM((2, half_rows, channels), BF16)],
            compiler_params=params(8),
            cost_estimate=cost(flops, 4 << 20),
            name="last" if last else "next",
        )(
            lhs, head, tail,
            swap(head, "row", 1),
            swap(tail, "row", 1),
            total,
        )
    return total.reshape(1, rows, cols, channels)


def solution(mesh):
    in_specs = (
        P("dp", "row", "col", None),
        P("dp", "row", "col"),
        P(),
        P(),
        P(None, "dp", None),
        P(),
        P(),
    )
    out_specs = P("dp", "row", "col", None)
    return jax.shard_map(local, mesh=mesh, in_specs=in_specs, out_specs=out_specs, check_vma=False)
```

time: 111 us -> 47.1 us (0.42)
  blocking collectives: 32.3 us -> 0 us
  Pallas kernels: 0 us -> 20.9 us
  between operations: 13.6 us -> 0.2 us
  matrix products: 13.2 us -> 0 us
  local copies, waits for them, and re-layouts: 8.69 us -> 0.05 us
  waiting for transfers between devices: 20.7 us -> 12.5 us
  other arithmetic: 6.5 us -> 0.37 us
  starting transfers between devices: 16.1 us -> 12.9 us
    psum x2 -> x0, blocking collectives: 32.3 us -> none  [the longest x1 18.5 us: local(): sums = lax.psum(jnp.sum(grouped, axis=(0, 1, 3)), ('row', 'col'))]
    pallas_call x0 -> x8, Pallas kernels: none -> 20.9 us  [the longest x1 8.89 us: local(): pl.pallas_call(functools.partial(windows_kernel, count, depth, half_rows,...]
    dot_general x1 -> x0, matrix products: 13.2 us -> none  [local(): jnp.dot(stacked, piece.reshape(9 * depth, piece.shape[2]), preferred_elem...]
    all_gather x1 -> x0, waiting for transfers between devices: 9.41 us -> none  [local(): piece = lax.all_gather(conv_weight, 'dp', axis=1, tiled=True)]
    unnamed x18 -> x14, local copies, waits for them, and re-layouts: 6.54 us -> 0.04 us
    unnamed x3 -> x0, other arithmetic: 4.01 us -> none
    ppermute x8 -> x15, starting transfers between devices: 16.1 us -> 12.9 us  [swap(): return lax.ppermute(value, axis, [(i, i ^ bit) for i in range(size)])]
    ppermute x8 -> x15, waiting for transfers between devices: 10.6 us -> 12.5 us  [swap(): return lax.ppermute(value, axis, [(i, i ^ bit) for i in range(size)])]
  transfers between devices with their start and end apart: 9 -> 15, of which waited for: 5 -> 6; matrix products, arithmetic and copies ran while one was open for 13% -> 1% of each run, Pallas kernels for 0% -> 33%
where the time goes in v1:
time: 47.1 us; the launch traced here: 46.9 us
  Pallas kernels  20.9 us (44%)
  starting transfers between devices  12.9 us (27%)
  waiting for transfers between devices  12.5 us (27%)
    ppermute x15, starting transfers between devices, swap(): return lax.ppermute(value, axis, [(i, i ^ bit) for i in range(size)])  12.9 us
    ppermute x15, waiting for transfers between devices, swap(): return lax.ppermute(value, axis, [(i, i ^ bit) for i in range(size)])  12.5 us
    pallas_call x1, Pallas kernels, local(): pl.pallas_call(functools.partial(windows_kernel, count, depth, half_rows,...  8.89 us
    pallas_call x3, Pallas kernels, local(): pl.pallas_call(functools.partial(next_kernel, stride, number + 1), out_sh...  8.57 us
    pallas_call x1, Pallas kernels, local(): pl.pallas_call(cut_kernel, out_shape=[jax.ShapeDtypeStruct((first, channe...  2.2 us
    pallas_call x1, Pallas kernels, local(): pl.pallas_call(functools.partial(stats_kernel, per_group), out_shape=[lin...  1.06 us
  transfers between devices with their start and end apart: 15, of which 6 were waited for; matrix products, arithmetic and copies ran while one was open for 1% of the time, Pallas kernels for 33%

profile of v1, /device:TPU:0, one launch (start us, length us, event | category | flops | bytes accessed | tf_op | source)
XLA Modules:
  0.0 46.9 jit_solution(11916156398662215720)
XLA Ops:
  0.0 2.2 %cut.1 = (bf16[384,640]{1,0:T(8,128)(2,1)}, bf16[336,640]{1,0:T(8,128)(2,1)}) custom-call(bf16[1440,640]{1,0:T(8,128)(2,1)} %bitcast.7), custom_call_target="tpu_custom_call" | custom-call | tf_op jit(solution)/shard_map/cut/pallas_call | solution.py:351
  2.3 3.0 %collective-permute-start.5 = (bf16[336,640]{1,0:T(8,128)(2,1)}, bf16[336,640]{1,0:T(8,128)(2,1)}, u32[]{:S(2)}, u32[]{:S(2)}) collective-permute-start(bf16[336,640]{1,0:T(8,128)(2,1)} %get-tuple-element.36), channel_id=1, source_target_pairs={{0,8},{8,0},{16,24},{24,16},{1,9},{9,1},{17,25},{25,17},{2,10},{10... | collective-permute-start | bytes 1290248 | tf_op jit(solution)/shard_map/ppermute | solution.py:26
  5.3 1.5 %collective-permute-start.3 = (bf16[384,640]{1,0:T(8,128)(2,1)}, bf16[384,640]{1,0:T(8,128)(2,1)S(1)}, u32[]{:S(2)}, u32[]{:S(2)}) collective-permute-start(bf16[384,640]{1,0:T(8,128)(2,1)} %get-tuple-element.38), channel_id=1, source_target_pairs={{0,16},{8,24},{16,0},{24,8},{1,17},{9,25},{17,1},{25,9},{2,18},{10... | collective-permute-start | bytes 1474568 | tf_op jit(solution)/shard_map/ppermute | solution.py:26
  6.9 0.3 fusion.member
  7.2 1.1 %stats.1 = (f32[48,640]{1,0:T(8,128)S(1)}, f32[48,640]{1,0:T(8,128)S(1)}, f32[8,128]{1,0:T(8,128)S(1)}) custom-call(bf16[20,40,640]{2,1,0:T(8,128)(2,1)S(1)} %bitcast.4, s32[20,1,40]{2,1,0:T(1,128)S(1)} %bitcast.9, bf16[640,128]{1,0:T(8,128)(2,1)S(1)} %fusion.member), custom_call_target="tpu_custom_call" | custom-call | bytes 4194304 | tf_op jit(solution)/shard_map/stats/pallas_call | solution.py:374
  8.4 0.6 %collective-permute-start.12 = (bf16[384,640]{1,0:T(8,128)(2,1)}, bf16[384,640]{1,0:T(8,128)(2,1)S(1)}, u32[]{:S(2)}, u32[]{:S(2)}) collective-permute-start(bf16[384,640]{1,0:T(8,128)(2,1)} %get-tuple-element.38), channel_id=1, source_target_pairs={{0,8},{8,0},{16,24},{24,16},{1,9},{9,1},{17,25},{25,17},{2,10},{10... | collective-permute-start | bytes 1474568 | tf_op jit(solution)/shard_map/ppermute | solution.py:26
  9.0 0.7 %collective-permute-done.above.below = f32[48,640]{1,0:T(8,128)S(1)} collective-permute-done((f32[48,640]{1,0:T(8,128)S(1)}, f32[48,640]{1,0:T(8,128)S(1)}, u32[]{:S(2)}, u32[]{:S(2)}) %collective-permute-start) | collective-permute-done | bytes 122912 | tf_op jit(solution)/shard_map/ppermute | solution.py:26
  9.7 0.1 message_one.1
  9.8 1.6 %collective-permute-start.1 = (bf16[48,768]{1,0:T(8,128)(2,1)S(1)}, bf16[48,768]{1,0:T(8,128)(2,1)S(1)}, u32[]{:S(2)}, u32[]{:S(2)}) collective-permute-start(bf16[48,768]{1,0:T(8,128)(2,1)S(1)} %get-tuple-element.26), channel_id=1, source_target_pairs={{0,1},{1,0},{2,3},{3,2},{4,5},{5,4},{6,7},{7,6},{8,9},{9,8},{10,11... | collective-permute-start | bytes 221192 | tf_op jit(solution)/shard_map/ppermute | solution.py:26
  11.5 2.8 %collective-permute-done.1.got.near = bf16[48,768]{1,0:T(8,128)(2,1)S(1)} collective-permute-done((bf16[48,768]{1,0:T(8,128)(2,1)S(1)}, bf16[48,768]{1,0:T(8,128)(2,1)S(1)}, u32[]{:S(2)}, u32[]{:S(2)}) %collective-permute-start.1) | collective-permute-done | bytes 73760 | tf_op jit(solution)/shard_map/ppermute | solution.py:26
  14.3 3.7 %collective-permute-start.2 = (bf16[48,768]{1,0:T(8,128)(2,1)S(1)}, bf16[48,768]{1,0:T(8,128)(2,1)S(1)}, u32[]{:S(2)}, u32[]{:S(2)}) collective-permute-start(bf16[48,768]{1,0:T(8,128)(2,1)S(1)} %get-tuple-element.29), channel_id=1, source_target_pairs={{0,3},{1,2},{2,1},{3,0},{4,7},{5,6},{6,5},{7,4},{8,11},{9,10},{10,... | collective-permute-start | bytes 221192 | tf_op jit(solution)/shard_map/ppermute | solution.py:26
  17.9 0.5 %collective-permute-start.9 = (bf16[336,640]{1,0:T(8,128)(2,1)}, bf16[336,640]{1,0:T(8,128)(2,1)S(1)}, u32[]{:S(2)}, u32[]{:S(2)}) collective-permute-start(bf16[336,640]{1,0:T(8,128)(2,1)} %get-tuple-element.36), channel_id=1, source_target_pairs={{0,16},{8,24},{16,0},{24,8},{1,17},{9,25},{17,1},{25,9},{2,18},{10... | collective-permute-start | bytes 1290248 | tf_op jit(solution)/shard_map/ppermute | solution.py:26
  18.5 2.1 %collective-permute-done.2.far = bf16[48,768]{1,0:T(8,128)(2,1)S(1)} collective-permute-done((bf16[48,768]{1,0:T(8,128)(2,1)S(1)}, bf16[48,768]{1,0:T(8,128)(2,1)S(1)}, u32[]{:S(2)}, u32[]{:S(2)}) %collective-permute-start.2) | collective-permute-done | bytes 73760 | tf_op jit(solution)/shard_map/ppermute | solution.py:26
  20.6 0.5 %collective-permute-start.6 = (bf16[336,640]{1,0:T(8,128)(2,1)}, bf16[336,640]{1,0:T(8,128)(2,1)S(1)}, u32[]{:S(2)}, u32[]{:S(2)}) collective-permute-start(bf16[336,640]{1,0:T(8,128)(2,1)} %collective-permute-done.5.two), channel_id=1, source_target_pairs={{0,16},{8,24},{16,0},{24,8},{1,17},{9,25},{17,1},{25,9},{2,18},{10... | collective-permute-start | bytes 1290248 | tf_op jit(solution)/shard_map/ppermute | solution.py:26
  21.1 0.8 %collective-permute-start.4 = (bf16[384,640]{1,0:T(8,128)(2,1)S(1)}, bf16[384,640]{1,0:T(8,128)(2,1)S(1)}, u32[]{:S(2)}, u32[]{:S(2)}) collective-permute-start(bf16[384,640]{1,0:T(8,128)(2,1)S(1)} %collective-permute-done.3.one), channel_id=1, source_target_pairs={{0,8},{8,0},{16,24},{24,16},{1,9},{9,1},{17,25},{25,17},{2,10},{10... | collective-permute-start | bytes 1474568 | tf_op jit(solution)/shard_map/ppermute | solution.py:26
  21.9 8.9 %windows.1 = (bf16[8,800,720]{2,1,0:T(8,128)(2,1)S(1)}, f32[800,640]{1,0:T(8,128)S(1)}) custom-call(bf16[20,40,640]{2,1,0:T(8,128)(2,1)S(1)} %bitcast.6, s32[20,1,40]{2,1,0:T(1,128)S(1)} %bitcast.11, f32[48,640]{1,0:T(8,128)S(1)} %collective-permute-done.above.below, f32[48,640]{1,0:T(8,128)S(1)} %collective-permute-done.above.below, ...), custom_call_target="tpu_custom_call" | custom-call | flops 2949120000 | bytes 25165824 | tf_op jit(solution)/shard_map/windows/pallas_call | solution.py:429
  30.8 0.1 collective-permute-done.9.two
  30.9 0.4 collective-permute-start.10
  31.4 0.1 collective-permute-start.11
  31.4 5.1 %collective-permute-done.4.one = bf16[384,640]{1,0:T(8,128)(2,1)S(1)} collective-permute-done((bf16[384,640]{1,0:T(8,128)(2,1)S(1)}, bf16[384,640]{1,0:T(8,128)(2,1)S(1)}, u32[]{:S(2)}, u32[]{:S(2)}) %collective-permute-start.4) | collective-permute-done | bytes 491552 | tf_op jit(solution)/shard_map/ppermute | solution.py:26
  36.5 1.8 %collective-permute-done.6.two = bf16[336,640]{1,0:T(8,128)(2,1)S(1)} collective-permute-done((bf16[336,640]{1,0:T(8,128)(2,1)}, bf16[336,640]{1,0:T(8,128)(2,1)S(1)}, u32[]{:S(2)}, u32[]{:S(2)}) %collective-permute-start.6) | collective-permute-done | bytes 430112 | tf_op jit(solution)/shard_map/ppermute | solution.py:26
  38.3 3.2 %next.2.total = f32[800,640]{1,0:T(8,128)S(1)} custom-call(bf16[8,800,720]{2,1,0:T(8,128)(2,1)S(1)} %get-tuple-element.31.lhs, bf16[384,640]{1,0:T(8,128)(2,1)S(1)} %collective-permute-done.12.one, bf16[336,640]{1,0:T(8,128)(2,1)} %collective-permute-done.5.two, bf16[384,640]{1,0:T(8,128)(2,1)S(1)} %collective-permute-done.13.three, ...), custom_call_target="tpu_custom_call" | custom-call | flops 1474560000 | bytes 4194304 | tf_op jit(solution)/shard_map/next/pallas_call | solution.py:454
  41.5 2.2 %next.3.total = f32[800,640]{1,0:T(8,128)S(1)} custom-call(bf16[8,800,720]{2,1,0:T(8,128)(2,1)S(1)} %get-tuple-element.31.lhs, bf16[384,640]{1,0:T(8,128)(2,1)S(1)} %collective-permute-done.3.one, bf16[336,640]{1,0:T(8,128)(2,1)S(1)} %collective-permute-done.9.two, bf16[384,640]{1,0:T(8,128)(2,1)S(1)} %collective-permute-done.10.three, ...), custom_call_target="tpu_custom_call" | custom-call | flops 1474560000 | bytes 4194304 | tf_op jit(solution)/shard_map/next/pallas_call | solution.py:454
  43.8 3.2 %last.1 = bf16[800,640]{1,0:T(8,128)(2,1)} custom-call(bf16[8,800,720]{2,1,0:T(8,128)(2,1)S(1)} %get-tuple-element.31.lhs, bf16[384,640]{1,0:T(8,128)(2,1)S(1)} %collective-permute-done.4.one, bf16[336,640]{1,0:T(8,128)(2,1)S(1)} %collective-permute-done.6.two, bf16[384,640]{1,0:T(8,128)(2,1)S(1)} %collective-permute-done.7.three, ...), custom_call_target="tpu_custom_call" | custom-call | flops 1474560000 | bytes 4194304 | tf_op jit(solution)/shard_map/last/pallas_call | solution.py:454
  (36 shorter events, 0.3 us)
Async XLA Ops:
  0.0 7.2 %copy-start = (bf16[1,20,40,640]{3,2,1,0:T(8,128)(2,1)S(1)}, bf16[1,20,40,640]{3,2,1,0:T(8,128)(2,1)}, u32[]{:S(2)}) copy-start(bf16[1,20,40,640]{3,2,1,0:T(8,128)(2,1)} %param.7) | copy-start | bytes 3072004
  0.0 7.2 %copy-start.2 = (s32[1,20,40]{2,0,1:T(1,128)S(1)}, s32[1,20,40]{2,0,1:T(1,128)}, u32[]{:S(2)}) copy-start(s32[1,20,40]{2,0,1:T(1,128)} %param.8) | copy-start | bytes 9604
  2.2 16.2 %copy-start.4 = (f32[640]{0:T(1024)S(1)}, f32[640]{0:T(1024)}, u32[]{:S(2)}) copy-start(f32[640]{0:T(1024)} %param.10) | copy-start | bytes 7684
  2.2 16.2 %copy-start.5 = (f32[640]{0:T(1024)S(1)}, f32[640]{0:T(1024)}, u32[]{:S(2)}) copy-start(f32[640]{0:T(1024)} %param.13) | copy-start | bytes 7684
  2.2 16.2 %copy-start.6 = (f32[640]{0:T(1024)S(1)}, f32[640]{0:T(1024)}, u32[]{:S(2)}) copy-start(f32[640]{0:T(1024)} %param.9) | copy-start | bytes 7684
  2.3 19.6 %copy-start.1 = (bf16[9,160,640]{2,1,0:T(8,128)(2,1)S(1)}, bf16[9,160,640]{2,1,0:T(8,128)(2,1)}, u32[]{:S(2)}) copy-start(bf16[9,160,640]{2,1,0:T(8,128)(2,1)} %param.11) | copy-start | bytes 5529604
  2.3 19.6 %copy-start.3 = (f32[9,640]{1,0:T(8,128)S(1)}, f32[9,640]{1,0:T(8,128)}, u32[]{:S(2)}) copy-start(f32[9,640]{1,0:T(8,128)} %mask_weight.1) | copy-start | bytes 69124
  2.3 18.3 %collective-permute-start.5 = (bf16[336,640]{1,0:T(8,128)(2,1)}, bf16[336,640]{1,0:T(8,128)(2,1)}, u32[]{:S(2)}, u32[]{:S(2)}) collective-permute-start(bf16[336,640]{1,0:T(8,128)(2,1)} %get-tuple-element.36), channel_id=1, source_target_pairs={{0,8},{8,0},{16,24},{24,16},{1,9},{9,1},{17,25},{25,17},{2,10},{10... | collective-permute-start | bytes 1290248 | tf_op jit(solution)/shard_map/ppermute | solution.py:26
  5.3 15.8 %collective-permute-start.3 = (bf16[384,640]{1,0:T(8,128)(2,1)}, bf16[384,640]{1,0:T(8,128)(2,1)S(1)}, u32[]{:S(2)}, u32[]{:S(2)}) collective-permute-start(bf16[384,640]{1,0:T(8,128)(2,1)} %get-tuple-element.38), channel_id=1, source_target_pairs={{0,16},{8,24},{16,0},{24,8},{1,17},{9,25},{17,1},{25,9},{2,18},{10... | collective-permute-start | bytes 1474568 | tf_op jit(solution)/shard_map/ppermute | solution.py:26
  8.3 1.4 %collective-permute-start = (f32[48,640]{1,0:T(8,128)S(1)}, f32[48,640]{1,0:T(8,128)S(1)}, u32[]{:S(2)}, u32[]{:S(2)}) collective-permute-start(f32[48,640]{1,0:T(8,128)S(1)} %broadcast_select_fusion), channel_id=1, source_target_pairs={{0,4},{4,0},{1,5},{5,1},{2,6},{6,2},{3,7},{7,3},{8,12},{12,8},{9,1... | collective-permute-start | bytes 368648 | tf_op jit(solution)/shard_map/ppermute | solution.py:26
  8.4 22.4 %collective-permute-start.12 = (bf16[384,640]{1,0:T(8,128)(2,1)}, bf16[384,640]{1,0:T(8,128)(2,1)S(1)}, u32[]{:S(2)}, u32[]{:S(2)}) collective-permute-start(bf16[384,640]{1,0:T(8,128)(2,1)} %get-tuple-element.38), channel_id=1, source_target_pairs={{0,8},{8,0},{16,24},{24,16},{1,9},{9,1},{17,25},{25,17},{2,10},{10... | collective-permute-start | bytes 1474568 | tf_op jit(solution)/shard_map/ppermute | solution.py:26
  9.8 4.4 %collective-permute-start.1 = (bf16[48,768]{1,0:T(8,128)(2,1)S(1)}, bf16[48,768]{1,0:T(8,128)(2,1)S(1)}, u32[]{:S(2)}, u32[]{:S(2)}) collective-permute-start(bf16[48,768]{1,0:T(8,128)(2,1)S(1)} %get-tuple-element.26), channel_id=1, source_target_pairs={{0,1},{1,0},{2,3},{3,2},{4,5},{5,4},{6,7},{7,6},{8,9},{9,8},{10,11... | collective-permute-start | bytes 221192 | tf_op jit(solution)/shard_map/ppermute | solution.py:26
  14.3 6.3 %collective-permute-start.2 = (bf16[48,768]{1,0:T(8,128)(2,1)S(1)}, bf16[48,768]{1,0:T(8,128)(2,1)S(1)}, u32[]{:S(2)}, u32[]{:S(2)}) collective-permute-start(bf16[48,768]{1,0:T(8,128)(2,1)S(1)} %get-tuple-element.29), channel_id=1, source_target_pairs={{0,3},{1,2},{2,1},{3,0},{4,7},{5,6},{6,5},{7,4},{8,11},{9,10},{10,... | collective-permute-start | bytes 221192 | tf_op jit(solution)/shard_map/ppermute | solution.py:26
  17.9 13.0 %collective-permute-start.9 = (bf16[336,640]{1,0:T(8,128)(2,1)}, bf16[336,640]{1,0:T(8,128)(2,1)S(1)}, u32[]{:S(2)}, u32[]{:S(2)}) collective-permute-start(bf16[336,640]{1,0:T(8,128)(2,1)} %get-tuple-element.36), channel_id=1, source_target_pairs={{0,16},{8,24},{16,0},{24,8},{1,17},{9,25},{17,1},{25,9},{2,18},{10... | collective-permute-start | bytes 1290248 | tf_op jit(solution)/shard_map/ppermute | solution.py:26
  20.6 10.8 %collective-permute-start.14 = (bf16[336,640]{1,0:T(8,128)(2,1)}, bf16[336,640]{1,0:T(8,128)(2,1)S(1)}, u32[]{:S(2)}, u32[]{:S(2)}) collective-permute-start(bf16[336,640]{1,0:T(8,128)(2,1)} %collective-permute-done.5.two), channel_id=1, source_target_pairs={{0,4},{4,0},{1,5},{5,1},{2,6},{6,2},{3,7},{7,3},{8,12},{12,8},{9,1... | collective-permute-start | bytes 1290248 | tf_op jit(solution)/shard_map/ppermute | solution.py:26
  20.6 17.7 %collective-permute-start.6 = (bf16[336,640]{1,0:T(8,128)(2,1)}, bf16[336,640]{1,0:T(8,128)(2,1)S(1)}, u32[]{:S(2)}, u32[]{:S(2)}) collective-permute-start(bf16[336,640]{1,0:T(8,128)(2,1)} %collective-permute-done.5.two), channel_id=1, source_target_pairs={{0,16},{8,24},{16,0},{24,8},{1,17},{9,25},{17,1},{25,9},{2,18},{10... | collective-permute-start | bytes 1290248 | tf_op jit(solution)/shard_map/ppermute | solution.py:26
  21.1 15.4 %collective-permute-start.4 = (bf16[384,640]{1,0:T(8,128)(2,1)S(1)}, bf16[384,640]{1,0:T(8,128)(2,1)S(1)}, u32[]{:S(2)}, u32[]{:S(2)}) collective-permute-start(bf16[384,640]{1,0:T(8,128)(2,1)S(1)} %collective-permute-done.3.one), channel_id=1, source_target_pairs={{0,8},{8,0},{16,24},{24,16},{1,9},{9,1},{17,25},{25,17},{2,10},{10... | collective-permute-start | bytes 1474568 | tf_op jit(solution)/shard_map/ppermute | solution.py:26
  30.8 7.5 %collective-permute-start.13 = (bf16[384,640]{1,0:T(8,128)(2,1)S(1)}, bf16[384,640]{1,0:T(8,128)(2,1)S(1)}, u32[]{:S(2)}, u32[]{:S(2)}) collective-permute-start(bf16[384,640]{1,0:T(8,128)(2,1)S(1)} %collective-permute-done.12.one), channel_id=1, source_target_pairs={{0,4},{4,0},{1,5},{5,1},{2,6},{6,2},{3,7},{7,3},{8,12},{12,8},{9,1... | collective-permute-start | bytes 1474568 | tf_op jit(solution)/shard_map/ppermute | solution.py:26
  30.9 10.6 %collective-permute-start.10 = (bf16[384,640]{1,0:T(8,128)(2,1)S(1)}, bf16[384,640]{1,0:T(8,128)(2,1)S(1)}, u32[]{:S(2)}, u32[]{:S(2)}) collective-permute-start(bf16[384,640]{1,0:T(8,128)(2,1)S(1)} %collective-permute-done.3.one), channel_id=1, source_target_pairs={{0,4},{4,0},{1,5},{5,1},{2,6},{6,2},{3,7},{7,3},{8,12},{12,8},{9,1... | collective-permute-start | bytes 1474568 | tf_op jit(solution)/shard_map/ppermute | solution.py:26
  31.4 10.2 %collective-permute-start.11 = (bf16[336,640]{1,0:T(8,128)(2,1)S(1)}, bf16[336,640]{1,0:T(8,128)(2,1)S(1)}, u32[]{:S(2)}, u32[]{:S(2)}) collective-permute-start(bf16[336,640]{1,0:T(8,128)(2,1)S(1)} %collective-permute-done.9.two), channel_id=1, source_target_pairs={{0,4},{4,0},{1,5},{5,1},{2,6},{6,2},{3,7},{7,3},{8,12},{12,8},{9,1... | collective-permute-start | bytes 1290248 | tf_op jit(solution)/shard_map/ppermute | solution.py:26
  36.5 7.3 %collective-permute-start.7 = (bf16[384,640]{1,0:T(8,128)(2,1)S(1)}, bf16[384,640]{1,0:T(8,128)(2,1)S(1)}, u32[]{:S(2)}, u32[]{:S(2)}) collective-permute-start(bf16[384,640]{1,0:T(8,128)(2,1)S(1)} %collective-permute-done.4.one), channel_id=1, source_target_pairs={{0,4},{4,0},{1,5},{5,1},{2,6},{6,2},{3,7},{7,3},{8,12},{12,8},{9,1... | collective-permute-start | bytes 1474568 | tf_op jit(solution)/shard_map/ppermute | solution.py:26
  38.3 5.4 %collective-permute-start.8 = (bf16[336,640]{1,0:T(8,128)(2,1)S(1)}, bf16[336,640]{1,0:T(8,128)(2,1)S(1)}, u32[]{:S(2)}, u32[]{:S(2)}) collective-permute-start(bf16[336,640]{1,0:T(8,128)(2,1)S(1)} %collective-permute-done.6.two), channel_id=1, source_target_pairs={{0,4},{4,0},{1,5},{5,1},{2,6},{6,2},{3,7},{7,3},{8,12},{12,8},{9,1... | collective-permute-start | bytes 1290248 | tf_op jit(solution)/shard_map/ppermute | solution.py:26

commit v2 on v1

v2 whole, which is shorter than its diff:
```python
import functools

import jax
import jax.numpy as jnp
from jax import lax
from jax.experimental import pallas as pl
from jax.experimental.pallas import tpu as pltpu
from jax.sharding import PartitionSpec as P


GROUPS = 32
EPS = 1e-05
TAPS = 9
PARTS = 4
LANES = 128


VMEM = pl.BlockSpec(memory_space=pltpu.VMEM)
HBM = pl.BlockSpec(memory_space=pltpu.HBM)
F32 = jnp.float32
BF16 = jnp.bfloat16


def swap(value, axis, bit):
    size = lax.axis_size(axis)
    return lax.ppermute(value, axis, [(i, i ^ bit) for i in range(size)])


def cross(value, bits):
    n_dp, n_row = lax.axis_size("dp"), lax.axis_size("row")
    pairs = [
        (d * n_row + r, (d ^ bits[r % 2]) * n_row + r) for d in range(n_dp) for r in range(n_row)
    ]
    return lax.ppermute(value, ("dp", "row"), pairs)


def shift(value, axis, step):
    size = lax.axis_size(axis)
    pairs = [(i, i + step) for i in range(size) if 0 <= i + step < size]
    return lax.ppermute(value, axis, pairs)


def after(value, *others):
    return lax.optimization_barrier((value, *others))[0]


def params(mib):
    return pltpu.CompilerParams(vmem_limit_bytes=mib << 20)


def cost(flops, size):
    return pl.CostEstimate(flops=flops, bytes_accessed=size, transcendentals=0)


def thirds(value):
    high = value.astype(BF16)
    rest = value - high.astype(F32)
    middle = rest.astype(BF16)
    low = (rest - middle.astype(F32)).astype(BF16)
    return high, middle, low


def exact_dot(value, ones, dims):
    total = None
    for piece in thirds(value):
        term = lax.dot_general(piece, ones, (dims, ((), ())), preferred_element_type=F32)
        total = term if total is None else total + term
    return total


def membership(channels, per_group):
    channel = lax.broadcasted_iota(jnp.int32, (channels, LANES), 0)
    low = lax.broadcasted_iota(jnp.int32, (channels, LANES), 1) * per_group
    return jnp.where((channel >= low) & (channel < low + per_group), 1.0, 0.0).astype(BF16)


def by_group(value, member):
    return exact_dot(jnp.broadcast_to(value, (16, value.shape[1])), member, ((1,), (0,)))[:1]


def by_channel(value, member):
    return exact_dot(jnp.broadcast_to(value, (16, value.shape[1])), member, ((1,), (1,)))[:1]


def merged(mean, spread, other_mean, other_spread, count):
    gap = mean - other_mean
    return (mean + other_mean) * 0.5, spread + other_spread + gap * gap * (count * 0.5)


def edges_kept(count_row, count_col):
    row, col = lax.axis_index("row"), lax.axis_index("col")
    inside = (row > 0, row < count_row - 1, col > 0, col < count_col - 1)
    return [jnp.where(flag, 1.0, 0.0).astype(F32) for flag in inside]


def even_col():
    return lax.rem(lax.axis_index("col"), 2) == 0


def spans(half, depth):
    full = depth // LANES * LANES
    taps = [half * 5 + t for t in range(TAPS // 2)]
    pieces = [(tap, 0, full) for tap in taps]
    pieces += [(tap, full, depth - full) for tap in taps]
    pieces.append((TAPS // 2, half * depth // 2, depth // 2))
    return pieces


def cut_kernel(flip, weight, *refs):
    outs, sems = refs[:-1], refs[-1]
    depth = weight.shape[1]
    for half in range(2):

        @pl.when(lax.rem(lax.axis_index("row"), 2) == half ^ flip)
        def _():
            which, at, copies = 0, 0, []
            for number, (tap, start, width) in enumerate(spans(half, depth)):
                if at == outs[which].shape[0]:
                    which, at = which + 1, 0
                copies.append(
                    pltpu.make_async_copy(
                        weight.at[tap, pl.ds(start, width)],
                        outs[which].at[pl.ds(at, width)],
                        sems.at[number],
                    )
                )
                at += width
            for copy in copies:
                copy.start()
            for copy in copies:
                copy.wait()


def regrouped(value):
    tiles = [value[:, t * LANES : (t + 1) * LANES] for t in range(5)]
    lane = lax.broadcasted_iota(jnp.int32, tiles[0].shape, 1)
    main = [tiles[0]]
    for part in range(1, PARTS):
        mixed = jnp.where(lane >= 32 * part, tiles[part], tiles[part + 1])
        main.append(pltpu.roll(mixed, LANES - 32 * part, 1))
    rest = tiles[4]
    for part in range(2, -1, -1):
        rest = jnp.where(lane < 32 * (part + 1), tiles[part + 1], rest)
    return jnp.concatenate(main + [rest], axis=1)


def stats_kernel(per_group, cells, mask, up, down, stats, holes, held, sem):
    fetch = pltpu.make_async_copy(mask, held, sem)
    fetch.start()
    rows, cols, channels = cells.shape
    count = float(rows * cols)
    member = membership(channels, per_group)
    total = jnp.zeros((cols, channels), F32)
    for r in range(rows):
        total = total + cells[r].astype(F32)
    sums = jnp.sum(total, axis=0, keepdims=True)
    mean = by_group(sums, member) * (1.0 / (count * per_group))
    wide = by_channel(mean, member)
    total = jnp.zeros((cols, channels), F32)
    for r in range(rows):
        away = cells[r].astype(F32) - wide
        total = total + away * away
    spread = by_group(jnp.sum(total, axis=0, keepdims=True), member)
    lines = lax.broadcasted_iota(jnp.int32, (8, LANES), 0)
    block = jnp.where(lines == 0, mean, jnp.where(lines == 1, spread, 0.0))
    stats[...] = block
    fetch.wait()
    marks = held[:, 0, :].astype(F32)
    holes[...] = marks
    for out, r in ((up, 0), (down, rows - 1)):
        out[:cols, :] = cells[r].astype(F32)
        out[cols:, :] = jnp.zeros((8, channels), F32)
        out[cols : cols + 8, :LANES] = block
        out[cols + 2 : cols + 3, :cols] = marks[r : r + 1, :]


def first_message_kernel(count, sizes, cells, mask, above, below, own, other, near, far, stats):
    rows, cols, channels = cells.shape
    base = stats_row(rows)
    keep = edges_kept(*sizes)
    mean, spread = merged(own[0:1], own[1:2], other[0:1], other[1:2], count)
    lines = lax.broadcasted_iota(jnp.int32, (8, LANES), 0)
    block = jnp.where(lines == 0, mean, jnp.where(lines == 1, spread, 0.0))
    stats[...] = block
    lane = lax.broadcasted_iota(jnp.int32, (rows + 2, LANES), 1)
    edges = []
    for c in (0, cols - 1):
        body = jnp.concatenate(
            [above[c : c + 1, :], cells[:, c, :].astype(F32), below[c : c + 1, :]], axis=0
        )
        holes = jnp.concatenate(
            [
                above[cols + 2 : cols + 3, c : c + 1] * keep[0],
                mask[:, c : c + 1],
                below[cols + 2 : cols + 3, c : c + 1] * keep[1],
            ],
            axis=0,
        )
        edges.append((body, jnp.where(lane == 0, jnp.broadcast_to(holes, lane.shape), 0.0)))
    even = even_col()
    for out, swapped in ((near, False), (far, True)):
        first, last = edges[0], edges[1]
        if swapped:
            first, last = last, first
        out[...] = jnp.zeros(out.shape, BF16)
        out[: rows + 2, :channels] = jnp.where(even, last[0], first[0]).astype(BF16)
        out[: rows + 2, channels:] = jnp.where(even, last[1], first[1]).astype(BF16)
    near[base : base + 8, :LANES] = packed(mean, spread)


def stats_row(rows):
    return -(-(rows + 2) // 16) * 16


def packed(mean, spread):
    return jnp.concatenate(
        [*thirds(mean), *thirds(spread), jnp.zeros((2, mean.shape[1]), BF16)], axis=0
    )


def unpacked(message, base):
    block = message[base : base + 16, :LANES].astype(F32)
    return block[0:1] + block[1:2] + block[2:3], block[3:4] + block[4:5] + block[5:6]


def second_message_kernel(rows, count, own, got, stats):
    base = stats_row(rows)
    mean, spread = merged(own[0:1], own[1:2], *unpacked(got, base), count)
    lines = lax.broadcasted_iota(jnp.int32, (8, LANES), 0)
    stats[...] = jnp.where(lines == 0, mean, jnp.where(lines == 1, spread, 0.0))


def kind_of(tap):
    return tap % 3 + (3 if tap // 3 == 1 else 0)


def windows_of(src, packs, group, part, half, low, high, begin=0, end=TAPS // 2 + 1):
    tiles = []
    for number in range(begin, end):
        tap = half * 5 + number
        if number == TAPS // 2:
            tiles.append(packs[2 * part + half, low:high, :])
        else:
            move = group if tap // 3 == 2 else 0
            tiles.append(src[kind_of(tap), part, low + move : high + move, :])
    return jnp.concatenate(tiles, axis=1)


def windows_kernel(
    count, depth, half_rows, sizes, stride, cells, mask, above, below, near, far, own, other, norm_gain, norm_shift, mask_weight, bias, weight, src, packs, total, rests, kept, holes, held,
):
    rows, cols, channels = cells.shape
    group = 2 * cols
    member = membership(channels, channels // GROUPS)
    mean, spread = merged(own[0:1], own[1:2], other[0:1], other[1:2], count)
    mean_row = by_channel(mean, member)
    gain_row = by_channel(lax.rsqrt(spread * (0.5 / count) + EPS), member) * norm_gain[...]
    offset_row = norm_shift[...]

    def act(x):
        v = (x.astype(F32) - mean_row) * gain_row + offset_row
        half = 0.5 * v
        return half + half * jnp.tanh(half)

    keep = edges_kept(*sizes)
    is_even = even_col()
    from_near = near[: rows + 2, :].astype(F32)
    from_far = far[: rows + 2, :].astype(F32)
    left = jnp.where(is_even, from_far, from_near)
    right = jnp.where(is_even, from_near, from_far)
    left_act = regrouped(act(left[:, :channels]) * keep[2])
    right_act = regrouped(act(right[:, :channels]) * keep[3])
    place = lax.broadcasted_iota(jnp.int32, (cols, channels), 0)

    tall = jnp.concatenate(
        [
            above[cols + 2 : cols + 3, :cols] * keep[0],
            mask[...],
            below[cols + 2 : cols + 3, :cols] * keep[1],
        ],
        axis=0,
    )
    tall = jnp.concatenate(
        [
            left[:, channels : channels + 1] * keep[2],
            tall,
            right[:, channels : channels + 1] * keep[3],
            jnp.zeros((rows + 2, LANES - cols - 2), F32),
        ],
        axis=1,
    )
    tall = jnp.concatenate([tall, jnp.zeros((LANES - rows - 2, LANES), F32)], axis=0)
    flipped = tall.T
    moved = [flipped[dx : dx + cols, :] for dx in range(3)]
    ones = jnp.ones((cols, 1), F32)

    def hole_row(r):
        once = jnp.concatenate([m[:, r : r + 3] for m in moved] + [ones], axis=1)
        return jnp.concatenate([once, once, once, jnp.zeros((cols, 2), F32)], axis=1)

    def row_of(r):
        if r == 0:
            value = act(above[:cols, :])
        elif r == rows + 1:
            value = act(below[:cols, :])
        else:
            value = act(cells[r - 1])
        value = regrouped(value)
        lo, hi = left_act[r : r + 1], right_act[r : r + 1]
        if r == 0 or r == rows + 1:
            edge = keep[0] if r == 0 else keep[1]
            value, lo, hi = value * edge, lo * edge, hi * edge
        before = jnp.where(place == 0, jnp.broadcast_to(lo, value.shape), pltpu.roll(value, 1, 0))
        behind = jnp.where(
            place == cols - 1, jnp.broadcast_to(hi, value.shape), pltpu.roll(value, cols - 1, 0)
        )
        return before, value, behind

    def put(kind, place, first, second):
        value = jnp.concatenate([first, second], axis=0).astype(BF16)
        low, high = place * group, (place + 1) * group
        for part in range(PARTS):
            src[kind, part, low:high, :] = value[:, part * LANES : (part + 1) * LANES]
        rests[kind, low:high, :] = value[:, PARTS * LANES :]

    for pair in range(rows // 2 + 1):
        one = row_of(2 * pair)
        two = row_of(2 * pair + 1)
        for dx in range(3):
            put(dx, pair, one[dx], two[dx])
            if pair:
                put(3 + dx, pair - 1, kept[dx], one[dx])
            kept[dx] = two[dx]
        if pair < rows // 2:
            holes[pair * group : (pair + 1) * group, :32] = jnp.concatenate(
                [hole_row(2 * pair), hole_row(2 * pair + 1)], axis=0
            ).astype(BF16)

    def fill(step, carry):
        at = pl.multiple_of(step * group, group)
        lane = lax.broadcasted_iota(jnp.int32, (group, LANES), 1)

        def rest_of(tap):
            start = at + (group if tap // 3 == 2 else 0)
            return rests[kind_of(tap), pl.ds(start, group), :]

        def turned(value, amount):
            return pltpu.roll(value, amount % LANES, 1) if amount % LANES else value

        for half in range(2):
            taps = [half * 5 + t for t in range(4)]
            ends = [rest_of(tap) for tap in taps]
            for part in range(PARTS):
                spot = 2 * part + half
                rest = turned(ends[3], 32 * (3 - part))
                for number in (2, 1, 0):
                    piece = turned(ends[number], 32 * (number - part))
                    rest = jnp.where(lane < 32 * (number + 1), piece, rest)
                packs[spot, pl.ds(at, group), :LANES] = rest
                final = src[4, part, pl.ds(at, group), :]
                if half:
                    extra = turned(rest_of(4), 48 - 32 * part)
                    final = jnp.where(lane < 48, turned(final, 48), extra)
                packs[spot, pl.ds(at, group), LANES:] = final[:, : half_rows - 5 * LANES]
        return carry

    lax.fori_loop(0, rows // 2, fill, 0)

    taps = mask_weight[...]
    order = [3 * (k % 3) + k // 3 for k in range(TAPS)]
    table = jnp.concatenate([taps[t : t + 1] for t in order] + [bias[...]], axis=0)
    table = jnp.concatenate([*thirds(table), jnp.zeros((2, channels), BF16)], axis=0)
    part = lax.axis_index("dp") // stride
    result = jnp.dot(holes[:, :32], table, preferred_element_type=F32)
    for half in range(2):
        at = 0
        for tap, start, width in spans(half, depth):
            held[half, at : at + width, :] = weight[tap, start : start + width, :]
            at += width
    for half in range(2):
        lhs = windows_of(src, packs, group, part, half, 0, rows * cols)
        result = result + jnp.dot(lhs, held[half], preferred_element_type=F32)
    total[...] = result


def next_kernel(stride, group, src, packs, one, two, three, four, total, out, held):
    cut = one.shape[0]
    part = lax.axis_index("dp") // stride
    core = lax.rem(lax.axis_index("row"), 2)
    for spot, head, tail in ((core, one, two), (1 - core, three, four)):
        held[spot, :cut, :] = head[...]
        held[spot, cut:, :] = tail[...]
    result = total[...]
    for half in range(2):
        lhs = windows_of(src, packs, group, part ^ (1 + half), half, 0, total.shape[0])
        result = result + jnp.dot(lhs, held[half], preferred_element_type=F32)
    out[...] = result


def head_kernel(stride, group, flip, src, packs, direct, passed, total, out, held):
    owner = (lax.axis_index("dp") // stride) ^ flip
    core = lax.rem(lax.axis_index("row"), 2)
    held[core] = direct[...]
    held[1 - core] = passed[...]
    end = direct.shape[0] // LANES
    result = total[...]
    for half in range(2):
        lhs = windows_of(src, packs, group, owner, half, 0, total.shape[0], 0, end)
        result = result + jnp.dot(lhs, held[half], preferred_element_type=F32)
    out[...] = result


def piece_kernel(stride, group, flips, side, begin, src, packs, piece, total, out):
    part = lax.axis_index("dp") // stride
    for half in range(2):

        @pl.when(lax.rem(lax.axis_index("row"), 2) == half ^ side)
        def _():
            owner = part ^ flips[half]
            lhs = windows_of(src, packs, group, owner, half, 0, total.shape[0], begin)
            out[...] = total[...] + jnp.dot(lhs, piece[...], preferred_element_type=F32)


def last_kernel(stride, group, flip, begin, src, packs, piece, total, out, done, sems):
    cells = total.shape[0]
    owner = (lax.axis_index("dp") // stride) ^ flip
    bounds = [0, 320, 560, 720, cells] if cells == 800 else [0, cells]
    for half in range(2):

        @pl.when(lax.rem(lax.axis_index("row"), 2) != half)
        def _():
            copies = []
            for number, (low, high) in enumerate(zip(bounds[:-1], bounds[1:])):
                lhs = windows_of(src, packs, group, owner, half, low, high, begin)
                done[low:high, :] = (
                    total[low:high, :] + jnp.dot(lhs, piece[...], preferred_element_type=F32)
                ).astype(BF16)
                copies.append(
                    pltpu.make_async_copy(
                        done.at[pl.ds(low, high - low)],
                        out.at[pl.ds(low, high - low)],
                        sems.at[number],
                    )
                )
                copies[-1].start()
            for copy in copies:
                copy.wait()


def local(features, hole_mask, norm_gain, norm_shift, conv_weight, mask_weight, conv_bias):
    rows, cols, channels = features.shape[1:]
    cells = rows * cols
    per_group = channels // GROUPS
    n_dp, n_row, n_col = lax.axis_size("dp"), lax.axis_size("row"), lax.axis_size("col")
    if n_col != 4 or rows % 2 or cols % 8 or channels != 5 * LANES:
        raise ValueError("unsupported sizes")
    stride = n_dp // PARTS
    at_dp, at_row = lax.axis_index("dp"), lax.axis_index("row")

    shard = conv_weight
    bit = 1
    while bit < stride:
        other = swap(shard, "dp", bit)
        upper = (at_dp // bit) % 2 == 1
        shard = jnp.concatenate(
            [jnp.where(upper, other, shard), jnp.where(upper, shard, other)], axis=1
        )
        bit *= 2
    depth = shard.shape[1]
    half_rows = TAPS * depth // 2
    first = -(-(half_rows // 2) // LANES) * LANES

    source = pltpu.with_memory_space_constraint(shard, pltpu.HBM)

    def cut(flip, sizes):
        return pl.pallas_call(
            functools.partial(cut_kernel, flip),
            out_shape=[pltpu.VMEM((size, channels), BF16) for size in sizes],
            in_specs=[HBM],
            out_specs=[VMEM] * len(sizes),
            scratch_shapes=[pltpu.SemaphoreType.DMA((TAPS,))],
            compiler_params=params(4),
            cost_estimate=cost(0, 2 << 20),
            name="cut",
        )(source)

    straight, turned = (stride, 2 * stride), (2 * stride, stride)
    piece_a, piece_b = cut(0, (first, half_rows - first))
    w_a = cross(piece_a, straight)
    w_b = cross(piece_b, straight)
    (piece_c,) = cut(1, (half_rows,))

    image = features[0]
    mask = hole_mask.reshape(rows, 1, cols)
    stats_shape = jax.ShapeDtypeStruct((8, LANES), F32)
    line_shape = jax.ShapeDtypeStruct((cols + 8, channels), F32)
    up, down, stats, holes = pl.pallas_call(
        functools.partial(stats_kernel, per_group),
        out_shape=[line_shape, line_shape, stats_shape, pltpu.VMEM((rows, cols), F32)],
        in_specs=[VMEM, HBM],
        out_specs=[VMEM] * 4,
        scratch_shapes=[pltpu.VMEM((rows, 1, cols), jnp.int32), pltpu.SemaphoreType.DMA],
        compiler_params=params(4),
        cost_estimate=cost(0, 4 << 20),
        name="stats",
    )(image, pltpu.with_memory_space_constraint(mask, pltpu.HBM))
    count = float(cells * per_group)
    if n_row == 2:
        above = below = swap(jnp.where(at_row == 0, down, up), "row", 1)
        other = above[cols : cols + 8, :LANES]
    else:
        above = shift(down, "row", 1)
        below = shift(up, "row", -1)
        bit = 1
        other = swap(stats, "row", bit)
        while 2 * bit < n_row:
            mean, spread = merged(stats[0], stats[1], other[0], other[1], count)
            stats = jnp.concatenate([mean[None], spread[None], jnp.zeros((6, LANES), F32)])
            count *= 2.0
            bit *= 2
            other = swap(stats, "row", bit)

    message = jax.ShapeDtypeStruct((stats_row(rows) + 16, channels + LANES), BF16)
    near, far, stats = pl.pallas_call(
        functools.partial(first_message_kernel, count, (n_row, n_col)),
        out_shape=[message, message, stats_shape],
        in_specs=[VMEM] * 6,
        out_specs=[VMEM] * 3,
        compiler_params=params(4),
        cost_estimate=cost(0, 1 << 20),
        name="message_one",
    )(image, holes, above, below, stats, other)
    w_c = cross(after(piece_c, near), straight)
    near = swap(near, "col", 1)
    far = lax.ppermute(far, "col", [(1, 2), (2, 1)])
    count *= 2.0
    stats = pl.pallas_call(
        functools.partial(second_message_kernel, rows, count),
        out_shape=stats_shape,
        in_specs=[VMEM] * 2,
        out_specs=VMEM,
        compiler_params=params(4),
        cost_estimate=cost(0, 1 << 18),
        name="message_two",
    )(stats, near)
    other = swap(stats, "col", 2)
    w_a, w_b = after(w_a, stats), after(w_b, stats)
    d_a = cross(w_a, turned)
    f_a, f_b = swap(w_a, "row", 1), swap(w_b, "row", 1)
    count *= 2.0

    flops = 4 * cells * half_rows * channels
    src, packs, total = pl.pallas_call(
        functools.partial(windows_kernel, count, depth, half_rows, (n_row, n_col), stride),
        out_shape=[
            pltpu.VMEM((6, PARTS, cells + 2 * cols, LANES), BF16),
            pltpu.VMEM((2 * PARTS, cells, half_rows - PARTS * LANES), BF16),
            pltpu.VMEM((cells, channels), F32),
        ],
        in_specs=[VMEM] * 13,
        out_specs=[VMEM] * 3,
        scratch_shapes=[
            pltpu.VMEM((6, cells + 2 * cols, LANES), BF16),
            pltpu.VMEM((3, cols, channels), F32),
            pltpu.VMEM((cells, LANES), BF16),
            pltpu.VMEM((2, half_rows, channels), BF16),
        ],
        compiler_params=params(14),
        cost_estimate=cost(2 * flops, 24 << 20),
        name="windows",
    )(
        image, holes, above, below, near, far, stats, other,
        norm_gain[None], norm_shift[None], mask_weight, conv_bias[None], shard,
    )

    d_b = cross(after(w_b, src), turned)
    f_c = swap(after(w_c, src), "row", 1)
    accumulated = pltpu.VMEM((cells, channels), F32)
    total = pl.pallas_call(
        functools.partial(next_kernel, stride, 2 * cols),
        out_shape=accumulated,
        in_specs=[VMEM] * 7,
        out_specs=VMEM,
        scratch_shapes=[pltpu.VMEM((2, half_rows, channels), BF16)],
        compiler_params=params(8),
        cost_estimate=cost(flops, 4 << 20),
        name="next",
    )(src, packs, w_a, w_b, f_a, f_b, total)

    def piece_call(flips, side, begin, piece, total):
        return pl.pallas_call(
            functools.partial(piece_kernel, stride, 2 * cols, flips, side, begin),
            out_shape=accumulated,
            in_specs=[VMEM] * 4,
            out_specs=VMEM,
            compiler_params=params(8),
            cost_estimate=cost(flops // 2, 4 << 20),
            name="piece",
        )(src, packs, piece, total)

    d_a = after(d_a, total)
    total = pl.pallas_call(
        functools.partial(head_kernel, stride, 2 * cols, 3),
        out_shape=accumulated,
        in_specs=[VMEM] * 5,
        out_specs=VMEM,
        scratch_shapes=[pltpu.VMEM((2, first, channels), BF16)],
        compiler_params=params(8),
        cost_estimate=cost(flops // 2, 4 << 20),
        name="head",
    )(src, packs, d_a, swap(d_a, "row", 1), total)
    total = piece_call((2, 1), 1, 0, w_c, total)
    total = piece_call((2, 1), 0, 0, f_c, total)
    total = piece_call((3, 3), 0, first // LANES, d_b, total)
    total = pl.pallas_call(
        functools.partial(last_kernel, stride, 2 * cols, 3, first // LANES),
        out_shape=jax.ShapeDtypeStruct((cells, channels), BF16),
        in_specs=[VMEM] * 4,
        out_specs=HBM,
        scratch_shapes=[
            pltpu.VMEM((cells, channels), BF16),
            pltpu.SemaphoreType.DMA((4,)),
        ],
        compiler_params=params(8),
        cost_estimate=cost(flops // 4, 4 << 20),
        name="last",
    )(src, packs, swap(d_b, "row", 1), total)
    return total.reshape(1, rows, cols, channels)


def solution(mesh):
    in_specs = (
        P("dp", "row", "col", None),
        P("dp", "row", "col"),
        P(),
        P(),
        P(None, "dp", None),
        P(),
        P(),
    )
    out_specs = P("dp", "row", "col", None)
    return jax.shard_map(local, mesh=mesh, in_specs=in_specs, out_specs=out_specs, check_vma=False)
```

time: 47.1 us -> 52.7 us (1.12)
  waiting for transfers between devices: 12.5 us -> 16.7 us
  starting transfers between devices: 12.9 us -> 14.6 us
  Pallas kernels: 20.9 us -> 19.5 us
  local copies, waits for them, and re-layouts: 0.05 us -> 1.26 us
    ppermute x0 -> x6, waiting for transfers between devices: none -> 14.6 us  [the longest x5 14.6 us: cross(): return lax.ppermute(value, ('dp', 'row'), pairs)]
    ppermute x15 -> x8, waiting for transfers between devices: 12.5 us -> 2.13 us  [swap(): return lax.ppermute(value, axis, [(i, i ^ bit) for i in range(size)])]
    ppermute x0 -> x6, starting transfers between devices: none -> 8.9 us  [the longest x5 8.24 us: cross(): return lax.ppermute(value, ('dp', 'row'), pairs)]
    ppermute x15 -> x8, starting transfers between devices: 12.9 us -> 5.68 us  [swap(): return lax.ppermute(value, axis, [(i, i ^ bit) for i in range(size)])]
    pallas_call x1, Pallas kernels: 8.89 us -> 7.08 us  [local(): pl.pallas_call(functools.partial(windows_kernel, count, depth, half_rows,...]
    unnamed x14, local copies, waits for them, and re-layouts: 0.04 us -> 1.25 us
    pallas_call x4 -> x8, Pallas kernels: 10.8 us -> 11.2 us  [the longest x3 3.31 us: piece_call(): pl.pallas_call(functools.partial(piece_kernel, stride, 2 * cols, flips, s...]
  transfers between devices with their start and end apart: 15 -> 14, of which waited for: 6 -> 4; matrix products, arithmetic and copies ran while one was open for 1% -> 0% of each run, Pallas kernels for 33% -> 32%
where the time goes in v2:
time: 52.7 us; the launch traced here: 52.5 us
  Pallas kernels  19.5 us (37%)
  waiting for transfers between devices  16.7 us (32%)
  starting transfers between devices  14.6 us (28%)
  local copies, waits for them, and re-layouts  1.26 us (2%)
    ppermute x5, waiting for transfers between devices, cross(): return lax.ppermute(value, ('dp', 'row'), pairs)  14.6 us
    ppermute x5, starting transfers between devices, cross(): return lax.ppermute(value, ('dp', 'row'), pairs)  8.24 us
    pallas_call x1, Pallas kernels, local(): pl.pallas_call(functools.partial(windows_kernel, count, depth, half_rows,...  7.08 us
    ppermute x8, starting transfers between devices, swap(): return lax.ppermute(value, axis, [(i, i ^ bit) for i in range(size)])  5.68 us
    pallas_call x3, Pallas kernels, piece_call(): pl.pallas_call(functools.partial(piece_kernel, stride, 2 * cols, flips, s...  3.31 us
    pallas_call x2, Pallas kernels, cut(): pl.pallas_call(functools.partial(cut_kernel, flip), out_shape=[pltpu.VMEM...  2.71 us
    pallas_call x1, Pallas kernels, local(): pl.pallas_call(functools.partial(next_kernel, stride, 2 * cols), out_shap...  2.23 us
    ppermute x8, waiting for transfers between devices, swap(): return lax.ppermute(value, axis, [(i, i ^ bit) for i in range(size)])  2.13 us
  transfers between devices with their start and end apart: 14, of which 4 were waited for; matrix products, arithmetic and copies ran while one was open for 0% of the time, Pallas kernels for 32%

profile of v2, /device:TPU:0, one launch (start us, length us, event | category | flops | bytes accessed | tf_op | source)
XLA Modules:
  0.0 52.5 jit_solution(9704357471774999339)
XLA Ops:
  0.0 1.2 %copy-done.1 = bf16[1,20,40,640]{3,2,1,0:T(8,128)(2,1)S(1)} copy-done((bf16[1,20,40,640]{3,2,1,0:T(8,128)(2,1)S(1)}, bf16[1,20,40,640]{3,2,1,0:T(8,128)(2,1)}, u32[]{:S(2)}) %copy-start.1) | copy-done | bytes 1024024
  1.2 1.2 %stats.1 = (f32[48,640]{1,0:T(8,128)S(1)}, f32[48,640]{1,0:T(8,128)S(1)}, f32[8,128]{1,0:T(8,128)S(1)}, f32[20,40]{1,0:T(8,128)S(1)}) custom-call(bf16[20,40,640]{2,1,0:T(8,128)(2,1)S(1)} %bitcast.3, s32[20,1,40]{2,1,0:T(1,128)} %bitcast.6), custom_call_target="tpu_custom_call" | custom-call | bytes 4194304 | tf_op jit(solution)/shard_map/stats/pallas_call | solution.py:497
  2.4 0.6 %collective-permute-start = (f32[48,640]{1,0:T(8,128)S(1)}, f32[48,640]{1,0:T(8,128)S(1)}, u32[]{:S(2)}, u32[]{:S(2)}) collective-permute-start(f32[48,640]{1,0:T(8,128)S(1)} %broadcast_select_fusion), channel_id=1, source_target_pairs={{0,4},{4,0},{1,5},{5,1},{2,6},{6,2},{3,7},{7,3},{8,12},{12,8},{9,1... | collective-permute-start | bytes 368648 | tf_op jit(solution)/shard_map/ppermute | solution.py:26
  3.0 1.4 %cut.3 = bf16[720,640]{1,0:T(8,128)(2,1)S(1)} custom-call(bf16[9,160,640]{2,1,0:T(8,128)(2,1)} %weight.5), custom_call_target="tpu_custom_call" | custom-call | bytes 2097152 | tf_op jit(solution)/shard_map/cut/pallas_call | solution.py:476
  4.6 2.6 %collective-permute-start.7 = (bf16[720,640]{1,0:T(8,128)(2,1)S(1)}, bf16[720,640]{1,0:T(8,128)(2,1)S(1)}, u32[]{:S(2)}, u32[]{:S(2)}) collective-permute-start(bf16[720,640]{1,0:T(8,128)(2,1)S(1)} %cut.3), channel_id=1, source_target_pairs={{0,8},{4,20},{8,0},{12,28},{16,24},{20,4},{24,16},{28,12},{1,9},{5... | collective-permute-start | bytes 2764808 | tf_op jit(solution)/shard_map/ppermute | solution.py:34
  7.1 1.4 %cut.2 = (bf16[384,640]{1,0:T(8,128)(2,1)S(1)}, bf16[336,640]{1,0:T(8,128)(2,1)S(1)}) custom-call(bf16[9,160,640]{2,1,0:T(8,128)(2,1)} %weight.5), custom_call_target="tpu_custom_call" | custom-call | bytes 2097152 | tf_op jit(solution)/shard_map/cut/pallas_call | solution.py:476
  8.7 1.9 %collective-permute-start.4 = (bf16[336,640]{1,0:T(8,128)(2,1)S(1)}, bf16[336,640]{1,0:T(8,128)(2,1)S(1)}, u32[]{:S(2)}, u32[]{:S(2)}) collective-permute-start(bf16[336,640]{1,0:T(8,128)(2,1)S(1)} %get-tuple-element.32), channel_id=1, source_target_pairs={{0,8},{4,20},{8,0},{12,28},{16,24},{20,4},{24,16},{28,12},{1,9},{5... | collective-permute-start | bytes 1290248 | tf_op jit(solution)/shard_map/ppermute | solution.py:34
  10.6 1.6 %collective-permute-start.1 = (bf16[48,768]{1,0:T(8,128)(2,1)S(1)}, bf16[48,768]{1,0:T(8,128)(2,1)S(1)}, u32[]{:S(2)}, u32[]{:S(2)}) collective-permute-start(bf16[48,768]{1,0:T(8,128)(2,1)S(1)} %get-tuple-element.27), channel_id=1, source_target_pairs={{0,1},{1,0},{2,3},{3,2},{4,5},{5,4},{6,7},{7,6},{8,9},{9,8},{10,11... | collective-permute-start | bytes 221192 | tf_op jit(solution)/shard_map/ppermute | solution.py:26
  12.2 0.7 %collective-permute-start.2 = (bf16[48,768]{1,0:T(8,128)(2,1)S(1)}, bf16[48,768]{1,0:T(8,128)(2,1)S(1)}, u32[]{:S(2)}, u32[]{:S(2)}) collective-permute-start(bf16[48,768]{1,0:T(8,128)(2,1)S(1)} %get-tuple-element.28), channel_id=1, source_target_pairs={{1,2},{2,1},{5,6},{6,5},{9,10},{10,9},{13,14},{14,13},{17,18},{18,... | collective-permute-start | bytes 221192 | tf_op jit(solution)/shard_map/ppermute | solution.py:535
  12.8 2.1 %collective-permute-done.1.got.near = bf16[48,768]{1,0:T(8,128)(2,1)S(1)} collective-permute-done((bf16[48,768]{1,0:T(8,128)(2,1)S(1)}, bf16[48,768]{1,0:T(8,128)(2,1)S(1)}, u32[]{:S(2)}, u32[]{:S(2)}) %collective-permute-start.1) | collective-permute-done | bytes 73760 | tf_op jit(solution)/shard_map/ppermute | solution.py:26
  15.0 8.9 %collective-permute-done.9.one = bf16[384,640]{1,0:T(8,128)(2,1)S(1)} collective-permute-done((bf16[384,640]{1,0:T(8,128)(2,1)S(1)}, bf16[384,640]{1,0:T(8,128)(2,1)S(1)}, u32[]{:S(2)}, u32[]{:S(2)}) %collective-permute-start.9) | collective-permute-done | bytes 491552 | tf_op jit(solution)/shard_map/ppermute | solution.py:34
  23.8 3.1 %collective-permute-start.3 = (f32[8,128]{1,0:T(8,128)S(1)}, f32[8,128]{1,0:T(8,128)S(1)}, u32[]{:S(2)}, u32[]{:S(2)}) collective-permute-start(f32[8,128]{1,0:T(8,128)S(1)} %message_two.1.own), channel_id=1, source_target_pairs={{0,2},{1,3},{2,0},{3,1},{4,6},{5,7},{6,4},{7,5},{8,10},{9,11},{10,... | collective-permute-start | bytes 12296 | tf_op jit(solution)/shard_map/ppermute | solution.py:26
  27.0 1.4 %collective-permute-done.4.two = bf16[336,640]{1,0:T(8,128)(2,1)S(1)} collective-permute-done((bf16[336,640]{1,0:T(8,128)(2,1)S(1)}, bf16[336,640]{1,0:T(8,128)(2,1)S(1)}, u32[]{:S(2)}, u32[]{:S(2)}) %collective-permute-start.4) | collective-permute-done | bytes 430112 | tf_op jit(solution)/shard_map/ppermute | solution.py:34
  28.4 2.0 %collective-permute-start.10 = (bf16[384,640]{1,0:T(8,128)(2,1)S(1)}, bf16[384,640]{1,0:T(8,128)(2,1)S(1)}, u32[]{:S(2)}, u32[]{:S(2)}) collective-permute-start(bf16[384,640]{1,0:T(8,128)(2,1)S(1)} %collective-permute-done.9.one), channel_id=1, source_target_pairs={{0,16},{4,12},{8,24},{12,4},{16,0},{20,28},{24,8},{28,20},{1,17},{... | collective-permute-start | bytes 1474568 | tf_op jit(solution)/shard_map/ppermute | solution.py:34
  30.5 7.1 %windows.1 = (bf16[6,4,880,128]{3,2,1,0:T(8,128)(2,1)S(1)}, bf16[8,800,208]{2,1,0:T(8,128)(2,1)S(1)}, f32[800,640]{1,0:T(8,128)S(1)}) custom-call(bf16[20,40,640]{2,1,0:T(8,128)(2,1)S(1)} %bitcast.5, f32[20,40]{1,0:T(8,128)S(1)} %get-tuple-element.23.mask, f32[48,640]{1,0:T(8,128)S(1)} %collective-permute-done.above.below, ...), custom_call_target="tpu_custom_call" | custom-call | flops 2949120000 | bytes 25165824 | tf_op jit(solution)/shard_map/windows/pallas_call | solution.py:553
  37.6 0.3 collective-permute-start.8
  37.9 1.5 %collective-permute-start.5 = (bf16[336,640]{1,0:T(8,128)(2,1)S(1)}, bf16[336,640]{1,0:T(8,128)(2,1)S(1)}, u32[]{:S(2)}, u32[]{:S(2)}) collective-permute-start(bf16[336,640]{1,0:T(8,128)(2,1)S(1)} %collective-permute-done.4.two), channel_id=1, source_target_pairs={{0,16},{4,12},{8,24},{12,4},{16,0},{20,28},{24,8},{28,20},{1,17},{... | collective-permute-start | bytes 1290248 | tf_op jit(solution)/shard_map/ppermute | solution.py:34
  39.4 2.2 %next.1.total = f32[800,640]{1,0:T(8,128)S(1)} custom-call(bf16[6,4,880,128]{3,2,1,0:T(8,128)(2,1)S(1)} %get-tuple-element.30.src, bf16[8,800,208]{2,1,0:T(8,128)(2,1)S(1)} %get-tuple-element.31.packs, bf16[384,640]{1,0:T(8,128)(2,1)S(1)} %collective-permute-done.9.one, bf16[336,640]{1,0:T(8,128)(2,1)S(1)} %collective-permute-done.4.two, ...), custom_call_target="tpu_custom_call" | custom-call | flops 1474560000 | bytes 4194304 | tf_op jit(solution)/shard_map/next/pallas_call | solution.py:579
  41.8 4.2 %collective-permute-done.5.piece = bf16[336,640]{1,0:T(8,128)(2,1)S(1)} collective-permute-done((bf16[336,640]{1,0:T(8,128)(2,1)S(1)}, bf16[336,640]{1,0:T(8,128)(2,1)S(1)}, u32[]{:S(2)}, u32[]{:S(2)}) %collective-permute-start.5) | collective-permute-done | bytes 430112 | tf_op jit(solution)/shard_map/ppermute | solution.py:34
  46.1 1.4 %head.1.total = f32[800,640]{1,0:T(8,128)S(1)} custom-call(bf16[6,4,880,128]{3,2,1,0:T(8,128)(2,1)S(1)} %get-tuple-element.30.src, bf16[8,800,208]{2,1,0:T(8,128)(2,1)S(1)} %get-tuple-element.31.packs, bf16[384,640]{1,0:T(8,128)(2,1)S(1)} %collective-permute-done.10.direct, bf16[384,640]{1,0:T(8,128)(2,1)S(1)} %collective-permute-done.13.passed, ...), custom_call_target="tpu_custom_call" | custom-call | flops 737280000 | bytes 4194304 | tf_op jit(solution)/shard_map/head/pallas_call | solution.py:602
  47.5 1.2 %piece.3.total = f32[800,640]{1,0:T(8,128)S(1)} custom-call(bf16[6,4,880,128]{3,2,1,0:T(8,128)(2,1)S(1)} %get-tuple-element.30.src, bf16[8,800,208]{2,1,0:T(8,128)(2,1)S(1)} %get-tuple-element.31.packs, bf16[720,640]{1,0:T(8,128)(2,1)S(1)} %collective-permute-done.7.piece, f32[800,640]{1,0:T(8,128)S(1)} %head.1.total), custom_call_target="tpu_custom_call" | custom-call | flops 737280000 | bytes 4194304 | tf_op jit(solution)/shard_map/piece/pallas_call | solution.py:591
  48.7 1.3 %piece.4.total = f32[800,640]{1,0:T(8,128)S(1)} custom-call(bf16[6,4,880,128]{3,2,1,0:T(8,128)(2,1)S(1)} %get-tuple-element.30.src, bf16[8,800,208]{2,1,0:T(8,128)(2,1)S(1)} %get-tuple-element.31.packs, bf16[720,640]{1,0:T(8,128)(2,1)S(1)} %collective-permute-done.8.piece, f32[800,640]{1,0:T(8,128)S(1)} %piece.3.total), custom_call_target="tpu_custom_call" | custom-call | flops 737280000 | bytes 4194304 | tf_op jit(solution)/shard_map/piece/pallas_call | solution.py:591
  50.1 0.8 %piece.5.total = f32[800,640]{1,0:T(8,128)S(1)} custom-call(bf16[6,4,880,128]{3,2,1,0:T(8,128)(2,1)S(1)} %get-tuple-element.30.src, bf16[8,800,208]{2,1,0:T(8,128)(2,1)S(1)} %get-tuple-element.31.packs, bf16[336,640]{1,0:T(8,128)(2,1)S(1)} %collective-permute-done.5.piece, f32[800,640]{1,0:T(8,128)S(1)} %piece.4.total), custom_call_target="tpu_custom_call" | custom-call | flops 737280000 | bytes 4194304 | tf_op jit(solution)/shard_map/piece/pallas_call | solution.py:591
  50.8 1.5 %last.1 = bf16[800,640]{1,0:T(8,128)(2,1)} custom-call(bf16[6,4,880,128]{3,2,1,0:T(8,128)(2,1)S(1)} %get-tuple-element.30.src, bf16[8,800,208]{2,1,0:T(8,128)(2,1)S(1)} %get-tuple-element.31.packs, bf16[336,640]{1,0:T(8,128)(2,1)S(1)} %collective-permute-done.6.piece, f32[800,640]{1,0:T(8,128)S(1)} %piece.5.total), custom_call_target="tpu_custom_call" | custom-call | flops 368640000 | bytes 4194304 | tf_op jit(solution)/shard_map/last/pallas_call | solution.py:615
  (35 shorter events, 0.6 us)
Async XLA Ops:
  0.0 1.2 %copy-start.1 = (bf16[1,20,40,640]{3,2,1,0:T(8,128)(2,1)S(1)}, bf16[1,20,40,640]{3,2,1,0:T(8,128)(2,1)}, u32[]{:S(2)}) copy-start(bf16[1,20,40,640]{3,2,1,0:T(8,128)(2,1)} %param.7) | copy-start | bytes 3072004
  1.2 3.2 %copy-start.2 = (bf16[1,20,40,640]{3,2,1,0:T(8,128)(2,1)S(1)}, bf16[1,20,40,640]{3,2,1,0:T(8,128)(2,1)}, u32[]{:S(2)}) copy-start(bf16[1,20,40,640]{3,2,1,0:T(8,128)(2,1)} %param.7) | copy-start | bytes 3072004
  2.4 2.0 %collective-permute-start = (f32[48,640]{1,0:T(8,128)S(1)}, f32[48,640]{1,0:T(8,128)S(1)}, u32[]{:S(2)}, u32[]{:S(2)}) collective-permute-start(f32[48,640]{1,0:T(8,128)S(1)} %broadcast_select_fusion), channel_id=1, source_target_pairs={{0,4},{4,0},{1,5},{5,1},{2,6},{6,2},{3,7},{7,3},{8,12},{12,8},{9,1... | collective-permute-start | bytes 368648 | tf_op jit(solution)/shard_map/ppermute | solution.py:26
  4.3 22.6 %copy-start.4 = (f32[640]{0:T(1024)S(1)}, f32[640]{0:T(1024)}, u32[]{:S(2)}) copy-start(f32[640]{0:T(1024)} %param.10) | copy-start | bytes 7684
  4.4 22.6 %copy-start.5 = (f32[640]{0:T(1024)S(1)}, f32[640]{0:T(1024)}, u32[]{:S(2)}) copy-start(f32[640]{0:T(1024)} %param.13) | copy-start | bytes 7684
  4.4 22.6 %copy-start.6 = (f32[640]{0:T(1024)S(1)}, f32[640]{0:T(1024)}, u32[]{:S(2)}) copy-start(f32[640]{0:T(1024)} %param.9) | copy-start | bytes 7684
  4.4 26.1 %copy-start = (bf16[9,160,640]{2,1,0:T(8,128)(2,1)S(1)}, bf16[9,160,640]{2,1,0:T(8,128)(2,1)}, u32[]{:S(2)}) copy-start(bf16[9,160,640]{2,1,0:T(8,128)(2,1)} %weight.5) | copy-start | bytes 5529604
  4.4 26.1 %copy-start.3 = (f32[9,640]{1,0:T(8,128)S(1)}, f32[9,640]{1,0:T(8,128)}, u32[]{:S(2)}) copy-start(f32[9,640]{1,0:T(8,128)} %mask_weight.1) | copy-start | bytes 69124
  4.6 33.0 %collective-permute-start.7 = (bf16[720,640]{1,0:T(8,128)(2,1)S(1)}, bf16[720,640]{1,0:T(8,128)(2,1)S(1)}, u32[]{:S(2)}, u32[]{:S(2)}) collective-permute-start(bf16[720,640]{1,0:T(8,128)(2,1)S(1)} %cut.3), channel_id=1, source_target_pairs={{0,8},{4,20},{8,0},{12,28},{16,24},{20,4},{24,16},{28,12},{1,9},{5... | collective-permute-start | bytes 2764808 | tf_op jit(solution)/shard_map/ppermute | solution.py:34
  8.5 15.3 %collective-permute-start.9 = (bf16[384,640]{1,0:T(8,128)(2,1)S(1)}, bf16[384,640]{1,0:T(8,128)(2,1)S(1)}, u32[]{:S(2)}, u32[]{:S(2)}) collective-permute-start(bf16[384,640]{1,0:T(8,128)(2,1)S(1)} %get-tuple-element.37), channel_id=1, source_target_pairs={{0,8},{4,20},{8,0},{12,28},{16,24},{20,4},{24,16},{28,12},{1,9},{5... | collective-permute-start | bytes 1474568 | tf_op jit(solution)/shard_map/ppermute | solution.py:34
  8.7 19.7 %collective-permute-start.4 = (bf16[336,640]{1,0:T(8,128)(2,1)S(1)}, bf16[336,640]{1,0:T(8,128)(2,1)S(1)}, u32[]{:S(2)}, u32[]{:S(2)}) collective-permute-start(bf16[336,640]{1,0:T(8,128)(2,1)S(1)} %get-tuple-element.32), channel_id=1, source_target_pairs={{0,8},{4,20},{8,0},{12,28},{16,24},{20,4},{24,16},{28,12},{1,9},{5... | collective-permute-start | bytes 1290248 | tf_op jit(solution)/shard_map/ppermute | solution.py:34
  10.6 4.4 %collective-permute-start.1 = (bf16[48,768]{1,0:T(8,128)(2,1)S(1)}, bf16[48,768]{1,0:T(8,128)(2,1)S(1)}, u32[]{:S(2)}, u32[]{:S(2)}) collective-permute-start(bf16[48,768]{1,0:T(8,128)(2,1)S(1)} %get-tuple-element.27), channel_id=1, source_target_pairs={{0,1},{1,0},{2,3},{3,2},{4,5},{5,4},{6,7},{7,6},{8,9},{9,8},{10,11... | collective-permute-start | bytes 221192 | tf_op jit(solution)/shard_map/ppermute | solution.py:26
  12.2 16.3 %collective-permute-start.2 = (bf16[48,768]{1,0:T(8,128)(2,1)S(1)}, bf16[48,768]{1,0:T(8,128)(2,1)S(1)}, u32[]{:S(2)}, u32[]{:S(2)}) collective-permute-start(bf16[48,768]{1,0:T(8,128)(2,1)S(1)} %get-tuple-element.28), channel_id=1, source_target_pairs={{1,2},{2,1},{5,6},{6,5},{9,10},{10,9},{13,14},{14,13},{17,18},{18,... | collective-permute-start | bytes 221192 | tf_op jit(solution)/shard_map/ppermute | solution.py:535
  23.8 15.6 %collective-permute-start.11 = (bf16[384,640]{1,0:T(8,128)(2,1)S(1)}, bf16[384,640]{1,0:T(8,128)(2,1)S(1)}, u32[]{:S(2)}, u32[]{:S(2)}) collective-permute-start(bf16[384,640]{1,0:T(8,128)(2,1)S(1)} %collective-permute-done.9.one), channel_id=1, source_target_pairs={{0,4},{4,0},{1,5},{5,1},{2,6},{6,2},{3,7},{7,3},{8,12},{12,8},{9,1... | collective-permute-start | bytes 1474568 | tf_op jit(solution)/shard_map/ppermute | solution.py:26
  23.8 6.7 %collective-permute-start.3 = (f32[8,128]{1,0:T(8,128)S(1)}, f32[8,128]{1,0:T(8,128)S(1)}, u32[]{:S(2)}, u32[]{:S(2)}) collective-permute-start(f32[8,128]{1,0:T(8,128)S(1)} %message_two.1.own), channel_id=1, source_target_pairs={{0,2},{1,3},{2,0},{3,1},{4,6},{5,7},{6,4},{7,5},{8,10},{9,11},{10,... | collective-permute-start | bytes 12296 | tf_op jit(solution)/shard_map/ppermute | solution.py:26
  28.4 11.0 %collective-permute-start.12 = (bf16[336,640]{1,0:T(8,128)(2,1)S(1)}, bf16[336,640]{1,0:T(8,128)(2,1)S(1)}, u32[]{:S(2)}, u32[]{:S(2)}) collective-permute-start(bf16[336,640]{1,0:T(8,128)(2,1)S(1)} %collective-permute-done.4.two), channel_id=1, source_target_pairs={{0,4},{4,0},{1,5},{5,1},{2,6},{6,2},{3,7},{7,3},{8,12},{12,8},{9,1... | collective-permute-start | bytes 1290248 | tf_op jit(solution)/shard_map/ppermute | solution.py:26
  28.4 13.2 %collective-permute-start.10 = (bf16[384,640]{1,0:T(8,128)(2,1)S(1)}, bf16[384,640]{1,0:T(8,128)(2,1)S(1)}, u32[]{:S(2)}, u32[]{:S(2)}) collective-permute-start(bf16[384,640]{1,0:T(8,128)(2,1)S(1)} %collective-permute-done.9.one), channel_id=1, source_target_pairs={{0,16},{4,12},{8,24},{12,4},{16,0},{20,28},{24,8},{28,20},{1,17},{... | collective-permute-start | bytes 1474568 | tf_op jit(solution)/shard_map/ppermute | solution.py:34
  37.6 11.1 %collective-permute-start.8 = (bf16[720,640]{1,0:T(8,128)(2,1)S(1)}, bf16[720,640]{1,0:T(8,128)(2,1)S(1)}, u32[]{:S(2)}, u32[]{:S(2)}) collective-permute-start(bf16[720,640]{1,0:T(8,128)(2,1)S(1)} %collective-permute-done.7.piece), channel_id=1, source_target_pairs={{0,4},{4,0},{1,5},{5,1},{2,6},{6,2},{3,7},{7,3},{8,12},{12,8},{9,1... | collective-permute-start | bytes 2764808 | tf_op jit(solution)/shard_map/ppermute | solution.py:26
  37.9 8.2 %collective-permute-start.5 = (bf16[336,640]{1,0:T(8,128)(2,1)S(1)}, bf16[336,640]{1,0:T(8,128)(2,1)S(1)}, u32[]{:S(2)}, u32[]{:S(2)}) collective-permute-start(bf16[336,640]{1,0:T(8,128)(2,1)S(1)} %collective-permute-done.4.two), channel_id=1, source_target_pairs={{0,16},{4,12},{8,24},{12,4},{16,0},{20,28},{24,8},{28,20},{1,17},{... | collective-permute-start | bytes 1290248 | tf_op jit(solution)/shard_map/ppermute | solution.py:34
  41.6 4.4 %collective-permute-start.13 = (bf16[384,640]{1,0:T(8,128)(2,1)S(1)}, bf16[384,640]{1,0:T(8,128)(2,1)S(1)}, u32[]{:S(2)}, u32[]{:S(2)}) collective-permute-start(bf16[384,640]{1,0:T(8,128)(2,1)S(1)} %collective-permute-done.10.direct), channel_id=1, source_target_pairs={{0,4},{4,0},{1,5},{5,1},{2,6},{6,2},{3,7},{7,3},{8,12},{12,8},{9,1... | collective-permute-start | bytes 1474568 | tf_op jit(solution)/shard_map/ppermute | solution.py:26
  46.0 4.8 %collective-permute-start.6 = (bf16[336,640]{1,0:T(8,128)(2,1)S(1)}, bf16[336,640]{1,0:T(8,128)(2,1)S(1)}, u32[]{:S(2)}, u32[]{:S(2)}) collective-permute-start(bf16[336,640]{1,0:T(8,128)(2,1)S(1)} %collective-permute-done.5.piece), channel_id=1, source_target_pairs={{0,4},{4,0},{1,5},{5,1},{2,6},{6,2},{3,7},{7,3},{8,12},{12,8},{9,1... | collective-permute-start | bytes 1290248 | tf_op jit(solution)/shard_map/ppermute | solution.py:26

commit v3 on v2

--- a/solution.py
+++ b/solution.py
@@ -350,12 +350,17 @@
         for half in range(2):
             taps = [half * 5 + t for t in range(4)]
             ends = [rest_of(tap) for tap in taps]
+            shifted = []
+            for amount in range(4):
+                mixed = ends[(3 + amount) % 4]
+                for part in (2, 1, 0):
+                    mixed = jnp.where(lane < 32 * (part + 1), ends[(part + amount) % 4], mixed)
+                shifted.append(turned(mixed, 32 * amount))
             for part in range(PARTS):
                 spot = 2 * part + half
-                rest = turned(ends[3], 32 * (3 - part))
+                rest = shifted[(3 - part) % 4]
                 for number in (2, 1, 0):
-                    piece = turned(ends[number], 32 * (number - part))
-                    rest = jnp.where(lane < 32 * (number + 1), piece, rest)
+                    rest = jnp.where(lane < 32 * (number + 1), shifted[(number - part) % 4], rest)
                 packs[spot, pl.ds(at, group), :LANES] = rest
                 final = src[4, part, pl.ds(at, group), :]
                 if half:
@@ -610,8 +615,8 @@
         name="head",
     )(src, packs, d_a, swap(d_a, "row", 1), total)
     total = piece_call((2, 1), 1, 0, w_c, total)
+    total = piece_call((3, 3), 0, first // LANES, d_b, total)
     total = piece_call((2, 1), 0, 0, f_c, total)
-    total = piece_call((3, 3), 0, first // LANES, d_b, total)
     total = pl.pallas_call(
         functools.partial(last_kernel, stride, 2 * cols, 3, first // LANES),
         out_shape=jax.ShapeDtypeStruct((cells, channels), BF16),

time: 52.7 us -> 54.5 us (1.034)
  waiting for transfers between devices: 16.7 us -> 19.5 us
  Pallas kernels: 19.5 us -> 18.8 us
    ppermute x5, waiting for transfers between devices: 14.6 us -> 16.7 us  [cross(): return lax.ppermute(value, ('dp', 'row'), pairs)]
    pallas_call x1, Pallas kernels: 7.08 us -> 6.28 us  [local(): pl.pallas_call(functools.partial(windows_kernel, count, depth, half_rows,...]
    ppermute x8, waiting for transfers between devices: 2.13 us -> 2.79 us  [swap(): return lax.ppermute(value, axis, [(i, i ^ bit) for i in range(size)])]
  transfers between devices with their start and end apart: 14 -> 14, of which waited for: 4 -> 4; matrix products, arithmetic and copies ran while one was open for 0% -> 0% of each run, Pallas kernels for 32% -> 29%
where the time goes in v3:
time: 54.5 us; the launch traced here: 54.3 us
  waiting for transfers between devices  19.5 us (36%)
  Pallas kernels  18.8 us (34%)
  starting transfers between devices  14.3 us (26%)
  local copies, waits for them, and re-layouts  1.26 us (2%)
    ppermute x5, waiting for transfers between devices, cross(): return lax.ppermute(value, ('dp', 'row'), pairs)  16.7 us
    ppermute x5, starting transfers between devices, cross(): return lax.ppermute(value, ('dp', 'row'), pairs)  8.09 us
    pallas_call x1, Pallas kernels, local(): pl.pallas_call(functools.partial(windows_kernel, count, depth, half_rows,...  6.28 us
    ppermute x8, starting transfers between devices, swap(): return lax.ppermute(value, axis, [(i, i ^ bit) for i in range(size)])  5.6 us
    pallas_call x3, Pallas kernels, piece_call(): pl.pallas_call(functools.partial(piece_kernel, stride, 2 * cols, flips, s...  3.33 us
    ppermute x8, waiting for transfers between devices, swap(): return lax.ppermute(value, axis, [(i, i ^ bit) for i in range(size)])  2.79 us
    pallas_call x2, Pallas kernels, cut(): pl.pallas_call(functools.partial(cut_kernel, flip), out_shape=[pltpu.VMEM...  2.71 us
    pallas_call x1, Pallas kernels, local(): pl.pallas_call(functools.partial(next_kernel, stride, 2 * cols), out_shap...  2.23 us
  transfers between devices with their start and end apart: 14, of which 4 were waited for; matrix products, arithmetic and copies ran while one was open for 0% of the time, Pallas kernels for 29%

profile of v3, /device:TPU:0, one launch (start us, length us, event | category | flops | bytes accessed | tf_op | source)
XLA Modules:
  0.0 54.3 jit_solution(6833334857622544660)
XLA Ops:
  0.0 1.2 %copy-done.1 = bf16[1,20,40,640]{3,2,1,0:T(8,128)(2,1)S(1)} copy-done((bf16[1,20,40,640]{3,2,1,0:T(8,128)(2,1)S(1)}, bf16[1,20,40,640]{3,2,1,0:T(8,128)(2,1)}, u32[]{:S(2)}) %copy-start.1) | copy-done | bytes 1024024
  1.2 1.2 %stats.1 = (f32[48,640]{1,0:T(8,128)S(1)}, f32[48,640]{1,0:T(8,128)S(1)}, f32[8,128]{1,0:T(8,128)S(1)}, f32[20,40]{1,0:T(8,128)S(1)}) custom-call(bf16[20,40,640]{2,1,0:T(8,128)(2,1)S(1)} %bitcast.3, s32[20,1,40]{2,1,0:T(1,128)} %bitcast.6), custom_call_target="tpu_custom_call" | custom-call | bytes 4194304 | tf_op jit(solution)/shard_map/stats/pallas_call | solution.py:502
  2.4 0.6 %collective-permute-start = (f32[48,640]{1,0:T(8,128)S(1)}, f32[48,640]{1,0:T(8,128)S(1)}, u32[]{:S(2)}, u32[]{:S(2)}) collective-permute-start(f32[48,640]{1,0:T(8,128)S(1)} %broadcast_select_fusion), channel_id=1, source_target_pairs={{0,4},{4,0},{1,5},{5,1},{2,6},{6,2},{3,7},{7,3},{8,12},{12,8},{9,1... | collective-permute-start | bytes 368648 | tf_op jit(solution)/shard_map/ppermute | solution.py:26
  3.0 1.4 %cut.3 = bf16[720,640]{1,0:T(8,128)(2,1)S(1)} custom-call(bf16[9,160,640]{2,1,0:T(8,128)(2,1)} %weight.5), custom_call_target="tpu_custom_call" | custom-call | bytes 2097152 | tf_op jit(solution)/shard_map/cut/pallas_call | solution.py:481
  4.6 2.6 %collective-permute-start.7 = (bf16[720,640]{1,0:T(8,128)(2,1)S(1)}, bf16[720,640]{1,0:T(8,128)(2,1)S(1)}, u32[]{:S(2)}, u32[]{:S(2)}) collective-permute-start(bf16[720,640]{1,0:T(8,128)(2,1)S(1)} %cut.3), channel_id=1, source_target_pairs={{0,8},{4,20},{8,0},{12,28},{16,24},{20,4},{24,16},{28,12},{1,9},{5... | collective-permute-start | bytes 2764808 | tf_op jit(solution)/shard_map/ppermute | solution.py:34
  7.1 1.4 %cut.2 = (bf16[384,640]{1,0:T(8,128)(2,1)S(1)}, bf16[336,640]{1,0:T(8,128)(2,1)S(1)}) custom-call(bf16[9,160,640]{2,1,0:T(8,128)(2,1)} %weight.5), custom_call_target="tpu_custom_call" | custom-call | bytes 2097152 | tf_op jit(solution)/shard_map/cut/pallas_call | solution.py:481
  8.7 1.9 %collective-permute-start.4 = (bf16[336,640]{1,0:T(8,128)(2,1)S(1)}, bf16[336,640]{1,0:T(8,128)(2,1)S(1)}, u32[]{:S(2)}, u32[]{:S(2)}) collective-permute-start(bf16[336,640]{1,0:T(8,128)(2,1)S(1)} %get-tuple-element.32), channel_id=1, source_target_pairs={{0,8},{4,20},{8,0},{12,28},{16,24},{20,4},{24,16},{28,12},{1,9},{5... | collective-permute-start | bytes 1290248 | tf_op jit(solution)/shard_map/ppermute | solution.py:34
  10.6 1.6 %collective-permute-start.1 = (bf16[48,768]{1,0:T(8,128)(2,1)S(1)}, bf16[48,768]{1,0:T(8,128)(2,1)S(1)}, u32[]{:S(2)}, u32[]{:S(2)}) collective-permute-start(bf16[48,768]{1,0:T(8,128)(2,1)S(1)} %get-tuple-element.27), channel_id=1, source_target_pairs={{0,1},{1,0},{2,3},{3,2},{4,5},{5,4},{6,7},{7,6},{8,9},{9,8},{10,11... | collective-permute-start | bytes 221192 | tf_op jit(solution)/shard_map/ppermute | solution.py:26
  12.2 2.8 %collective-permute-done.1.got.near = bf16[48,768]{1,0:T(8,128)(2,1)S(1)} collective-permute-done((bf16[48,768]{1,0:T(8,128)(2,1)S(1)}, bf16[48,768]{1,0:T(8,128)(2,1)S(1)}, u32[]{:S(2)}, u32[]{:S(2)}) %collective-permute-start.1) | collective-permute-done | bytes 73760 | tf_op jit(solution)/shard_map/ppermute | solution.py:26
  15.0 8.9 %collective-permute-done.9.one = bf16[384,640]{1,0:T(8,128)(2,1)S(1)} collective-permute-done((bf16[384,640]{1,0:T(8,128)(2,1)S(1)}, bf16[384,640]{1,0:T(8,128)(2,1)S(1)}, u32[]{:S(2)}, u32[]{:S(2)}) %collective-permute-start.9) | collective-permute-done | bytes 491552 | tf_op jit(solution)/shard_map/ppermute | solution.py:34
  23.8 0.7 %collective-permute-start.2 = (bf16[48,768]{1,0:T(8,128)(2,1)S(1)}, bf16[48,768]{1,0:T(8,128)(2,1)S(1)}, u32[]{:S(2)}, u32[]{:S(2)}) collective-permute-start(bf16[48,768]{1,0:T(8,128)(2,1)S(1)} %get-tuple-element.28), channel_id=1, source_target_pairs={{1,2},{2,1},{5,6},{6,5},{9,10},{10,9},{13,14},{14,13},{17,18},{18,... | collective-permute-start | bytes 221192 | tf_op jit(solution)/shard_map/ppermute | solution.py:540
  24.5 3.9 %collective-permute-done.4.two = bf16[336,640]{1,0:T(8,128)(2,1)S(1)} collective-permute-done((bf16[336,640]{1,0:T(8,128)(2,1)S(1)}, bf16[336,640]{1,0:T(8,128)(2,1)S(1)}, u32[]{:S(2)}, u32[]{:S(2)}) %collective-permute-start.4) | collective-permute-done | bytes 430112 | tf_op jit(solution)/shard_map/ppermute | solution.py:34
  28.4 3.1 %collective-permute-start.3 = (f32[8,128]{1,0:T(8,128)S(1)}, f32[8,128]{1,0:T(8,128)S(1)}, u32[]{:S(2)}, u32[]{:S(2)}) collective-permute-start(f32[8,128]{1,0:T(8,128)S(1)} %message_two.1.own), channel_id=1, source_target_pairs={{0,2},{1,3},{2,0},{3,1},{4,6},{5,7},{6,4},{7,5},{8,10},{9,11},{10,... | collective-permute-start | bytes 12296 | tf_op jit(solution)/shard_map/ppermute | solution.py:26
  31.6 1.6 %collective-permute-start.10 = (bf16[384,640]{1,0:T(8,128)(2,1)S(1)}, bf16[384,640]{1,0:T(8,128)(2,1)S(1)}, u32[]{:S(2)}, u32[]{:S(2)}) collective-permute-start(bf16[384,640]{1,0:T(8,128)(2,1)S(1)} %collective-permute-done.9.one), channel_id=1, source_target_pairs={{0,16},{4,12},{8,24},{12,4},{16,0},{20,28},{24,8},{28,20},{1,17},{... | collective-permute-start | bytes 1474568 | tf_op jit(solution)/shard_map/ppermute | solution.py:34
  33.2 6.3 %windows.1 = (bf16[6,4,880,128]{3,2,1,0:T(8,128)(2,1)S(1)}, bf16[8,800,208]{2,1,0:T(8,128)(2,1)S(1)}, f32[800,640]{1,0:T(8,128)S(1)}) custom-call(bf16[20,40,640]{2,1,0:T(8,128)(2,1)S(1)} %bitcast.5, f32[20,40]{1,0:T(8,128)S(1)} %get-tuple-element.23.mask, f32[48,640]{1,0:T(8,128)S(1)} %collective-permute-done.above.below, ...), custom_call_target="tpu_custom_call" | custom-call | flops 2949120000 | bytes 25165824 | tf_op jit(solution)/shard_map/windows/pallas_call | solution.py:558
  39.6 1.8 %collective-permute-start.5 = (bf16[336,640]{1,0:T(8,128)(2,1)S(1)}, bf16[336,640]{1,0:T(8,128)(2,1)S(1)}, u32[]{:S(2)}, u32[]{:S(2)}) collective-permute-start(bf16[336,640]{1,0:T(8,128)(2,1)S(1)} %collective-permute-done.4.two), channel_id=1, source_target_pairs={{0,16},{4,12},{8,24},{12,4},{16,0},{20,28},{24,8},{28,20},{1,17},{... | collective-permute-start | bytes 1290248 | tf_op jit(solution)/shard_map/ppermute | solution.py:34
  41.4 2.2 %next.1.total = f32[800,640]{1,0:T(8,128)S(1)} custom-call(bf16[6,4,880,128]{3,2,1,0:T(8,128)(2,1)S(1)} %get-tuple-element.30.src, bf16[8,800,208]{2,1,0:T(8,128)(2,1)S(1)} %get-tuple-element.31.packs, bf16[384,640]{1,0:T(8,128)(2,1)S(1)} %collective-permute-done.9.one, bf16[336,640]{1,0:T(8,128)(2,1)S(1)} %collective-permute-done.4.two, ...), custom_call_target="tpu_custom_call" | custom-call | flops 1474560000 | bytes 4194304 | tf_op jit(solution)/shard_map/next/pallas_call | solution.py:584
  43.7 0.3 collective-permute-start.13
  43.9 3.9 %collective-permute-done.5.piece = bf16[336,640]{1,0:T(8,128)(2,1)S(1)} collective-permute-done((bf16[336,640]{1,0:T(8,128)(2,1)S(1)}, bf16[336,640]{1,0:T(8,128)(2,1)S(1)}, u32[]{:S(2)}, u32[]{:S(2)}) %collective-permute-start.5) | collective-permute-done | bytes 430112 | tf_op jit(solution)/shard_map/ppermute | solution.py:34
  47.8 1.4 %head.1.total = f32[800,640]{1,0:T(8,128)S(1)} custom-call(bf16[6,4,880,128]{3,2,1,0:T(8,128)(2,1)S(1)} %get-tuple-element.30.src, bf16[8,800,208]{2,1,0:T(8,128)(2,1)S(1)} %get-tuple-element.31.packs, bf16[384,640]{1,0:T(8,128)(2,1)S(1)} %collective-permute-done.10.direct, bf16[384,640]{1,0:T(8,128)(2,1)S(1)} %collective-permute-done.13.passed, ...), custom_call_target="tpu_custom_call" | custom-call | flops 737280000 | bytes 4194304 | tf_op jit(solution)/shard_map/head/pallas_call | solution.py:607
  49.3 1.2 %piece.3.total = f32[800,640]{1,0:T(8,128)S(1)} custom-call(bf16[6,4,880,128]{3,2,1,0:T(8,128)(2,1)S(1)} %get-tuple-element.30.src, bf16[8,800,208]{2,1,0:T(8,128)(2,1)S(1)} %get-tuple-element.31.packs, bf16[720,640]{1,0:T(8,128)(2,1)S(1)} %collective-permute-done.7.piece, f32[800,640]{1,0:T(8,128)S(1)} %head.1.total), custom_call_target="tpu_custom_call" | custom-call | flops 737280000 | bytes 4194304 | tf_op jit(solution)/shard_map/piece/pallas_call | solution.py:596
  50.5 0.9 %piece.4.total = f32[800,640]{1,0:T(8,128)S(1)} custom-call(bf16[6,4,880,128]{3,2,1,0:T(8,128)(2,1)S(1)} %get-tuple-element.30.src, bf16[8,800,208]{2,1,0:T(8,128)(2,1)S(1)} %get-tuple-element.31.packs, bf16[336,640]{1,0:T(8,128)(2,1)S(1)} %collective-permute-done.5.piece, f32[800,640]{1,0:T(8,128)S(1)} %piece.3.total), custom_call_target="tpu_custom_call" | custom-call | flops 737280000 | bytes 4194304 | tf_op jit(solution)/shard_map/piece/pallas_call | solution.py:596
  51.4 1.2 %piece.5.total = f32[800,640]{1,0:T(8,128)S(1)} custom-call(bf16[6,4,880,128]{3,2,1,0:T(8,128)(2,1)S(1)} %get-tuple-element.30.src, bf16[8,800,208]{2,1,0:T(8,128)(2,1)S(1)} %get-tuple-element.31.packs, bf16[720,640]{1,0:T(8,128)(2,1)S(1)} %collective-permute-done.8.piece, f32[800,640]{1,0:T(8,128)S(1)} %piece.4.total), custom_call_target="tpu_custom_call" | custom-call | flops 737280000 | bytes 4194304 | tf_op jit(solution)/shard_map/piece/pallas_call | solution.py:596
  52.6 1.5 %last.1 = bf16[800,640]{1,0:T(8,128)(2,1)} custom-call(bf16[6,4,880,128]{3,2,1,0:T(8,128)(2,1)S(1)} %get-tuple-element.30.src, bf16[8,800,208]{2,1,0:T(8,128)(2,1)S(1)} %get-tuple-element.31.packs, bf16[336,640]{1,0:T(8,128)(2,1)S(1)} %collective-permute-done.6.piece, f32[800,640]{1,0:T(8,128)S(1)} %piece.5.total), custom_call_target="tpu_custom_call" | custom-call | flops 368640000 | bytes 4194304 | tf_op jit(solution)/shard_map/last/pallas_call | solution.py:620
  (35 shorter events, 0.5 us)
Async XLA Ops:
  0.0 1.2 %copy-start.1 = (bf16[1,20,40,640]{3,2,1,0:T(8,128)(2,1)S(1)}, bf16[1,20,40,640]{3,2,1,0:T(8,128)(2,1)}, u32[]{:S(2)}) copy-start(bf16[1,20,40,640]{3,2,1,0:T(8,128)(2,1)} %param.7) | copy-start | bytes 3072004
  1.2 3.2 %copy-start.2 = (bf16[1,20,40,640]{3,2,1,0:T(8,128)(2,1)S(1)}, bf16[1,20,40,640]{3,2,1,0:T(8,128)(2,1)}, u32[]{:S(2)}) copy-start(bf16[1,20,40,640]{3,2,1,0:T(8,128)(2,1)} %param.7) | copy-start | bytes 3072004
  2.4 2.0 %collective-permute-start = (f32[48,640]{1,0:T(8,128)S(1)}, f32[48,640]{1,0:T(8,128)S(1)}, u32[]{:S(2)}, u32[]{:S(2)}) collective-permute-start(f32[48,640]{1,0:T(8,128)S(1)} %broadcast_select_fusion), channel_id=1, source_target_pairs={{0,4},{4,0},{1,5},{5,1},{2,6},{6,2},{3,7},{7,3},{8,12},{12,8},{9,1... | collective-permute-start | bytes 368648 | tf_op jit(solution)/shard_map/ppermute | solution.py:26
  4.3 27.2 %copy-start.4 = (f32[640]{0:T(1024)S(1)}, f32[640]{0:T(1024)}, u32[]{:S(2)}) copy-start(f32[640]{0:T(1024)} %param.10) | copy-start | bytes 7684
  4.4 27.2 %copy-start.5 = (f32[640]{0:T(1024)S(1)}, f32[640]{0:T(1024)}, u32[]{:S(2)}) copy-start(f32[640]{0:T(1024)} %param.13) | copy-start | bytes 7684
  4.4 27.2 %copy-start.6 = (f32[640]{0:T(1024)S(1)}, f32[640]{0:T(1024)}, u32[]{:S(2)}) copy-start(f32[640]{0:T(1024)} %param.9) | copy-start | bytes 7684
  4.4 28.8 %copy-start = (bf16[9,160,640]{2,1,0:T(8,128)(2,1)S(1)}, bf16[9,160,640]{2,1,0:T(8,128)(2,1)}, u32[]{:S(2)}) copy-start(bf16[9,160,640]{2,1,0:T(8,128)(2,1)} %weight.5) | copy-start | bytes 5529604
  4.4 28.8 %copy-start.3 = (f32[9,640]{1,0:T(8,128)S(1)}, f32[9,640]{1,0:T(8,128)}, u32[]{:S(2)}) copy-start(f32[9,640]{1,0:T(8,128)} %mask_weight.1) | copy-start | bytes 69124
  4.6 34.9 %collective-permute-start.7 = (bf16[720,640]{1,0:T(8,128)(2,1)S(1)}, bf16[720,640]{1,0:T(8,128)(2,1)S(1)}, u32[]{:S(2)}, u32[]{:S(2)}) collective-permute-start(bf16[720,640]{1,0:T(8,128)(2,1)S(1)} %cut.3), channel_id=1, source_target_pairs={{0,8},{4,20},{8,0},{12,28},{16,24},{20,4},{24,16},{28,12},{1,9},{5... | collective-permute-start | bytes 2764808 | tf_op jit(solution)/shard_map/ppermute | solution.py:34
  8.5 15.3 %collective-permute-start.9 = (bf16[384,640]{1,0:T(8,128)(2,1)S(1)}, bf16[384,640]{1,0:T(8,128)(2,1)S(1)}, u32[]{:S(2)}, u32[]{:S(2)}) collective-permute-start(bf16[384,640]{1,0:T(8,128)(2,1)S(1)} %get-tuple-element.37), channel_id=1, source_target_pairs={{0,8},{4,20},{8,0},{12,28},{16,24},{20,4},{24,16},{28,12},{1,9},{5... | collective-permute-start | bytes 1474568 | tf_op jit(solution)/shard_map/ppermute | solution.py:34
  8.7 19.7 %collective-permute-start.4 = (bf16[336,640]{1,0:T(8,128)(2,1)S(1)}, bf16[336,640]{1,0:T(8,128)(2,1)S(1)}, u32[]{:S(2)}, u32[]{:S(2)}) collective-permute-start(bf16[336,640]{1,0:T(8,128)(2,1)S(1)} %get-tuple-element.32), channel_id=1, source_target_pairs={{0,8},{4,20},{8,0},{12,28},{16,24},{20,4},{24,16},{28,12},{1,9},{5... | collective-permute-start | bytes 1290248 | tf_op jit(solution)/shard_map/ppermute | solution.py:34
  10.6 4.4 %collective-permute-start.1 = (bf16[48,768]{1,0:T(8,128)(2,1)S(1)}, bf16[48,768]{1,0:T(8,128)(2,1)S(1)}, u32[]{:S(2)}, u32[]{:S(2)}) collective-permute-start(bf16[48,768]{1,0:T(8,128)(2,1)S(1)} %get-tuple-element.27), channel_id=1, source_target_pairs={{0,1},{1,0},{2,3},{3,2},{4,5},{5,4},{6,7},{7,6},{8,9},{9,8},{10,11... | collective-permute-start | bytes 221192 | tf_op jit(solution)/shard_map/ppermute | solution.py:26
  23.8 17.6 %collective-permute-start.11 = (bf16[384,640]{1,0:T(8,128)(2,1)S(1)}, bf16[384,640]{1,0:T(8,128)(2,1)S(1)}, u32[]{:S(2)}, u32[]{:S(2)}) collective-permute-start(bf16[384,640]{1,0:T(8,128)(2,1)S(1)} %collective-permute-done.9.one), channel_id=1, source_target_pairs={{0,4},{4,0},{1,5},{5,1},{2,6},{6,2},{3,7},{7,3},{8,12},{12,8},{9,1... | collective-permute-start | bytes 1474568 | tf_op jit(solution)/shard_map/ppermute | solution.py:26
  23.8 7.8 %collective-permute-start.2 = (bf16[48,768]{1,0:T(8,128)(2,1)S(1)}, bf16[48,768]{1,0:T(8,128)(2,1)S(1)}, u32[]{:S(2)}, u32[]{:S(2)}) collective-permute-start(bf16[48,768]{1,0:T(8,128)(2,1)S(1)} %get-tuple-element.28), channel_id=1, source_target_pairs={{1,2},{2,1},{5,6},{6,5},{9,10},{10,9},{13,14},{14,13},{17,18},{18,... | collective-permute-start | bytes 221192 | tf_op jit(solution)/shard_map/ppermute | solution.py:540
  28.4 13.0 %collective-permute-start.12 = (bf16[336,640]{1,0:T(8,128)(2,1)S(1)}, bf16[336,640]{1,0:T(8,128)(2,1)S(1)}, u32[]{:S(2)}, u32[]{:S(2)}) collective-permute-start(bf16[336,640]{1,0:T(8,128)(2,1)S(1)} %collective-permute-done.4.two), channel_id=1, source_target_pairs={{0,4},{4,0},{1,5},{5,1},{2,6},{6,2},{3,7},{7,3},{8,12},{12,8},{9,1... | collective-permute-start | bytes 1290248 | tf_op jit(solution)/shard_map/ppermute | solution.py:26
  28.4 4.8 %collective-permute-start.3 = (f32[8,128]{1,0:T(8,128)S(1)}, f32[8,128]{1,0:T(8,128)S(1)}, u32[]{:S(2)}, u32[]{:S(2)}) collective-permute-start(f32[8,128]{1,0:T(8,128)S(1)} %message_two.1.own), channel_id=1, source_target_pairs={{0,2},{1,3},{2,0},{3,1},{4,6},{5,7},{6,4},{7,5},{8,10},{9,11},{10,... | collective-permute-start | bytes 12296 | tf_op jit(solution)/shard_map/ppermute | solution.py:26
  31.6 12.0 %collective-permute-start.10 = (bf16[384,640]{1,0:T(8,128)(2,1)S(1)}, bf16[384,640]{1,0:T(8,128)(2,1)S(1)}, u32[]{:S(2)}, u32[]{:S(2)}) collective-permute-start(bf16[384,640]{1,0:T(8,128)(2,1)S(1)} %collective-permute-done.9.one), channel_id=1, source_target_pairs={{0,16},{4,12},{8,24},{12,4},{16,0},{20,28},{24,8},{28,20},{1,17},{... | collective-permute-start | bytes 1474568 | tf_op jit(solution)/shard_map/ppermute | solution.py:34
  39.5 11.9 %collective-permute-start.8 = (bf16[720,640]{1,0:T(8,128)(2,1)S(1)}, bf16[720,640]{1,0:T(8,128)(2,1)S(1)}, u32[]{:S(2)}, u32[]{:S(2)}) collective-permute-start(bf16[720,640]{1,0:T(8,128)(2,1)S(1)} %collective-permute-done.7.piece), channel_id=1, source_target_pairs={{0,4},{4,0},{1,5},{5,1},{2,6},{6,2},{3,7},{7,3},{8,12},{12,8},{9,1... | collective-permute-start | bytes 2764808 | tf_op jit(solution)/shard_map/ppermute | solution.py:26
  39.6 8.2 %collective-permute-start.5 = (bf16[336,640]{1,0:T(8,128)(2,1)S(1)}, bf16[336,640]{1,0:T(8,128)(2,1)S(1)}, u32[]{:S(2)}, u32[]{:S(2)}) collective-permute-start(bf16[336,640]{1,0:T(8,128)(2,1)S(1)} %collective-permute-done.4.two), channel_id=1, source_target_pairs={{0,16},{4,12},{8,24},{12,4},{16,0},{20,28},{24,8},{28,20},{1,17},{... | collective-permute-start | bytes 1290248 | tf_op jit(solution)/shard_map/ppermute | solution.py:34
  43.7 4.2 %collective-permute-start.13 = (bf16[384,640]{1,0:T(8,128)(2,1)S(1)}, bf16[384,640]{1,0:T(8,128)(2,1)S(1)}, u32[]{:S(2)}, u32[]{:S(2)}) collective-permute-start(bf16[384,640]{1,0:T(8,128)(2,1)S(1)} %collective-permute-done.10.direct), channel_id=1, source_target_pairs={{0,4},{4,0},{1,5},{5,1},{2,6},{6,2},{3,7},{7,3},{8,12},{12,8},{9,1... | collective-permute-start | bytes 1474568 | tf_op jit(solution)/shard_map/ppermute | solution.py:26
  47.8 4.8 %collective-permute-start.6 = (bf16[336,640]{1,0:T(8,128)(2,1)S(1)}, bf16[336,640]{1,0:T(8,128)(2,1)S(1)}, u32[]{:S(2)}, u32[]{:S(2)}) collective-permute-start(bf16[336,640]{1,0:T(8,128)(2,1)S(1)} %collective-permute-done.5.piece), channel_id=1, source_target_pairs={{0,4},{4,0},{1,5},{5,1},{2,6},{6,2},{3,7},{7,3},{8,12},{12,8},{9,1... | collective-permute-start | bytes 1290248 | tf_op jit(solution)/shard_map/ppermute | solution.py:26

commit v4 on v3

--- a/solution.py
+++ b/solution.py
@@ -402,27 +402,14 @@
     out[...] = result
 
 
-def head_kernel(stride, group, flip, src, packs, direct, passed, total, out, held):
-    owner = (lax.axis_index("dp") // stride) ^ flip
-    core = lax.rem(lax.axis_index("row"), 2)
-    held[core] = direct[...]
-    held[1 - core] = passed[...]
-    end = direct.shape[0] // LANES
-    result = total[...]
-    for half in range(2):
-        lhs = windows_of(src, packs, group, owner, half, 0, total.shape[0], 0, end)
-        result = result + jnp.dot(lhs, held[half], preferred_element_type=F32)
-    out[...] = result
-
-
-def piece_kernel(stride, group, flips, side, begin, src, packs, piece, total, out):
+def piece_kernel(stride, group, flips, side, begin, end, src, packs, piece, total, out):
     part = lax.axis_index("dp") // stride
     for half in range(2):
 
         @pl.when(lax.rem(lax.axis_index("row"), 2) == half ^ side)
         def _():
             owner = part ^ flips[half]
-            lhs = windows_of(src, packs, group, owner, half, 0, total.shape[0], begin)
+            lhs = windows_of(src, packs, group, owner, half, 0, total.shape[0], begin, end)
             out[...] = total[...] + jnp.dot(lhs, piece[...], preferred_element_type=F32)
 
 
@@ -592,9 +579,9 @@
         name="next",
     )(src, packs, w_a, w_b, f_a, f_b, total)
 
-    def piece_call(flips, side, begin, piece, total):
+    def piece_call(flips, side, begin, piece, total, end=TAPS // 2 + 1):
         return pl.pallas_call(
-            functools.partial(piece_kernel, stride, 2 * cols, flips, side, begin),
+            functools.partial(piece_kernel, stride, 2 * cols, flips, side, begin, end),
             out_shape=accumulated,
             in_specs=[VMEM] * 4,
             out_specs=VMEM,
@@ -604,16 +591,9 @@
         )(src, packs, piece, total)
 
     d_a = after(d_a, total)
-    total = pl.pallas_call(
-        functools.partial(head_kernel, stride, 2 * cols, 3),
-        out_shape=accumulated,
-        in_specs=[VMEM] * 5,
-        out_specs=VMEM,
-        scratch_shapes=[pltpu.VMEM((2, first, channels), BF16)],
-        compiler_params=params(8),
-        cost_estimate=cost(flops // 2, 4 << 20),
-        name="head",
-    )(src, packs, d_a, swap(d_a, "row", 1), total)
+    passed = swap(d_a, "row", 1)
+    total = piece_call((3, 3), 0, 0, d_a, total, first // LANES)
+    total = piece_call((3, 3), 1, 0, passed, total, first // LANES)
     total = piece_call((2, 1), 1, 0, w_c, total)
     total = piece_call((3, 3), 0, first // LANES, d_b, total)
     total = piece_call((2, 1), 0, 0, f_c, total)

time: 54.5 us -> 54.6 us (level)
    pallas_call x3 -> x5, Pallas kernels: 3.33 us -> 4.85 us  [piece_call(): pl.pallas_call(functools.partial(piece_kernel, stride, 2 * cols, flips, s...]
    pallas_call x1 -> x0, Pallas kernels: 1.42 us -> none  [local(): pl.pallas_call(functools.partial(head_kernel, stride, 2 * cols, 3), out_s...]
  transfers between devices with their start and end apart: 14 -> 14, of which waited for: 4 -> 4; matrix products, arithmetic and copies ran while one was open for 0% -> 0% of each run, Pallas kernels for 29% -> 30%
where the time goes in v4:
time: 54.6 us; the launch traced here: 54.4 us
  waiting for transfers between devices  19.5 us (36%)
  Pallas kernels  18.9 us (35%)
  starting transfers between devices  14.3 us (26%)
  local copies, waits for them, and re-layouts  1.26 us (2%)
    ppermute x5, waiting for transfers between devices, cross(): return lax.ppermute(value, ('dp', 'row'), pairs)  16.7 us
    ppermute x5, starting transfers between devices, cross(): return lax.ppermute(value, ('dp', 'row'), pairs)  8.09 us
    pallas_call x1, Pallas kernels, local(): pl.pallas_call(functools.partial(windows_kernel, count, depth, half_rows,...  6.28 us
    ppermute x8, starting transfers between devices, swap(): return lax.ppermute(value, axis, [(i, i ^ bit) for i in range(size)])  5.6 us
    pallas_call x5, Pallas kernels, piece_call(): pl.pallas_call(functools.partial(piece_kernel, stride, 2 * cols, flips, s...  4.85 us
    ppermute x8, waiting for transfers between devices, swap(): return lax.ppermute(value, axis, [(i, i ^ bit) for i in range(size)])  2.79 us
    pallas_call x2, Pallas kernels, cut(): pl.pallas_call(functools.partial(cut_kernel, flip), out_shape=[pltpu.VMEM...  2.71 us
    pallas_call x1, Pallas kernels, local(): pl.pallas_call(functools.partial(next_kernel, stride, 2 * cols), out_shap...  2.23 us
  transfers between devices with their start and end apart: 14, of which 4 were waited for; matrix products, arithmetic and copies ran while one was open for 0% of the time, Pallas kernels for 30%

profile of v4, /device:TPU:0, one launch (start us, length us, event | category | flops | bytes accessed | tf_op | source)
XLA Modules:
  0.0 54.4 jit_solution(11481485586691008238)
XLA Ops:
  0.0 1.2 %copy-done.1 = bf16[1,20,40,640]{3,2,1,0:T(8,128)(2,1)S(1)} copy-done((bf16[1,20,40,640]{3,2,1,0:T(8,128)(2,1)S(1)}, bf16[1,20,40,640]{3,2,1,0:T(8,128)(2,1)}, u32[]{:S(2)}) %copy-start.1) | copy-done | bytes 1024024
  1.2 1.2 %stats.1 = (f32[48,640]{1,0:T(8,128)S(1)}, f32[48,640]{1,0:T(8,128)S(1)}, f32[8,128]{1,0:T(8,128)S(1)}, f32[20,40]{1,0:T(8,128)S(1)}) custom-call(bf16[20,40,640]{2,1,0:T(8,128)(2,1)S(1)} %bitcast.3, s32[20,1,40]{2,1,0:T(1,128)} %bitcast.6), custom_call_target="tpu_custom_call" | custom-call | bytes 4194304 | tf_op jit(solution)/shard_map/stats/pallas_call | solution.py:489
  2.4 0.6 %collective-permute-start = (f32[48,640]{1,0:T(8,128)S(1)}, f32[48,640]{1,0:T(8,128)S(1)}, u32[]{:S(2)}, u32[]{:S(2)}) collective-permute-start(f32[48,640]{1,0:T(8,128)S(1)} %broadcast_select_fusion), channel_id=1, source_target_pairs={{0,4},{4,0},{1,5},{5,1},{2,6},{6,2},{3,7},{7,3},{8,12},{12,8},{9,1... | collective-permute-start | bytes 368648 | tf_op jit(solution)/shard_map/ppermute | solution.py:26
  3.0 1.4 %cut.3 = bf16[720,640]{1,0:T(8,128)(2,1)S(1)} custom-call(bf16[9,160,640]{2,1,0:T(8,128)(2,1)} %weight.5), custom_call_target="tpu_custom_call" | custom-call | bytes 2097152 | tf_op jit(solution)/shard_map/cut/pallas_call | solution.py:468
  4.6 2.6 %collective-permute-start.7 = (bf16[720,640]{1,0:T(8,128)(2,1)S(1)}, bf16[720,640]{1,0:T(8,128)(2,1)S(1)}, u32[]{:S(2)}, u32[]{:S(2)}) collective-permute-start(bf16[720,640]{1,0:T(8,128)(2,1)S(1)} %cut.3), channel_id=1, source_target_pairs={{0,8},{4,20},{8,0},{12,28},{16,24},{20,4},{24,16},{28,12},{1,9},{5... | collective-permute-start | bytes 2764808 | tf_op jit(solution)/shard_map/ppermute | solution.py:34
  7.1 1.4 %cut.2 = (bf16[384,640]{1,0:T(8,128)(2,1)S(1)}, bf16[336,640]{1,0:T(8,128)(2,1)S(1)}) custom-call(bf16[9,160,640]{2,1,0:T(8,128)(2,1)} %weight.5), custom_call_target="tpu_custom_call" | custom-call | bytes 2097152 | tf_op jit(solution)/shard_map/cut/pallas_call | solution.py:468
  8.7 1.9 %collective-permute-start.4 = (bf16[336,640]{1,0:T(8,128)(2,1)S(1)}, bf16[336,640]{1,0:T(8,128)(2,1)S(1)}, u32[]{:S(2)}, u32[]{:S(2)}) collective-permute-start(bf16[336,640]{1,0:T(8,128)(2,1)S(1)} %get-tuple-element.32), channel_id=1, source_target_pairs={{0,8},{4,20},{8,0},{12,28},{16,24},{20,4},{24,16},{28,12},{1,9},{5... | collective-permute-start | bytes 1290248 | tf_op jit(solution)/shard_map/ppermute | solution.py:34
  10.6 1.6 %collective-permute-start.1 = (bf16[48,768]{1,0:T(8,128)(2,1)S(1)}, bf16[48,768]{1,0:T(8,128)(2,1)S(1)}, u32[]{:S(2)}, u32[]{:S(2)}) collective-permute-start(bf16[48,768]{1,0:T(8,128)(2,1)S(1)} %get-tuple-element.27), channel_id=1, source_target_pairs={{0,1},{1,0},{2,3},{3,2},{4,5},{5,4},{6,7},{7,6},{8,9},{9,8},{10,11... | collective-permute-start | bytes 221192 | tf_op jit(solution)/shard_map/ppermute | solution.py:26
  12.2 2.8 %collective-permute-done.1.got.near = bf16[48,768]{1,0:T(8,128)(2,1)S(1)} collective-permute-done((bf16[48,768]{1,0:T(8,128)(2,1)S(1)}, bf16[48,768]{1,0:T(8,128)(2,1)S(1)}, u32[]{:S(2)}, u32[]{:S(2)}) %collective-permute-start.1) | collective-permute-done | bytes 73760 | tf_op jit(solution)/shard_map/ppermute | solution.py:26
  15.0 8.9 %collective-permute-done.9.one = bf16[384,640]{1,0:T(8,128)(2,1)S(1)} collective-permute-done((bf16[384,640]{1,0:T(8,128)(2,1)S(1)}, bf16[384,640]{1,0:T(8,128)(2,1)S(1)}, u32[]{:S(2)}, u32[]{:S(2)}) %collective-permute-start.9) | collective-permute-done | bytes 491552 | tf_op jit(solution)/shard_map/ppermute | solution.py:34
  23.8 0.7 %collective-permute-start.2 = (bf16[48,768]{1,0:T(8,128)(2,1)S(1)}, bf16[48,768]{1,0:T(8,128)(2,1)S(1)}, u32[]{:S(2)}, u32[]{:S(2)}) collective-permute-start(bf16[48,768]{1,0:T(8,128)(2,1)S(1)} %get-tuple-element.28), channel_id=1, source_target_pairs={{1,2},{2,1},{5,6},{6,5},{9,10},{10,9},{13,14},{14,13},{17,18},{18,... | collective-permute-start | bytes 221192 | tf_op jit(solution)/shard_map/ppermute | solution.py:527
  24.5 3.9 %collective-permute-done.4.two = bf16[336,640]{1,0:T(8,128)(2,1)S(1)} collective-permute-done((bf16[336,640]{1,0:T(8,128)(2,1)S(1)}, bf16[336,640]{1,0:T(8,128)(2,1)S(1)}, u32[]{:S(2)}, u32[]{:S(2)}) %collective-permute-start.4) | collective-permute-done | bytes 430112 | tf_op jit(solution)/shard_map/ppermute | solution.py:34
  28.4 3.1 %collective-permute-start.3 = (f32[8,128]{1,0:T(8,128)S(1)}, f32[8,128]{1,0:T(8,128)S(1)}, u32[]{:S(2)}, u32[]{:S(2)}) collective-permute-start(f32[8,128]{1,0:T(8,128)S(1)} %message_two.1.own), channel_id=1, source_target_pairs={{0,2},{1,3},{2,0},{3,1},{4,6},{5,7},{6,4},{7,5},{8,10},{9,11},{10,... | collective-permute-start | bytes 12296 | tf_op jit(solution)/shard_map/ppermute | solution.py:26
  31.6 1.6 %collective-permute-start.10 = (bf16[384,640]{1,0:T(8,128)(2,1)S(1)}, bf16[384,640]{1,0:T(8,128)(2,1)S(1)}, u32[]{:S(2)}, u32[]{:S(2)}) collective-permute-start(bf16[384,640]{1,0:T(8,128)(2,1)S(1)} %collective-permute-done.9.one), channel_id=1, source_target_pairs={{0,16},{4,12},{8,24},{12,4},{16,0},{20,28},{24,8},{28,20},{1,17},{... | collective-permute-start | bytes 1474568 | tf_op jit(solution)/shard_map/ppermute | solution.py:34
  33.2 6.3 %windows.1 = (bf16[6,4,880,128]{3,2,1,0:T(8,128)(2,1)S(1)}, bf16[8,800,208]{2,1,0:T(8,128)(2,1)S(1)}, f32[800,640]{1,0:T(8,128)S(1)}) custom-call(bf16[20,40,640]{2,1,0:T(8,128)(2,1)S(1)} %bitcast.5, f32[20,40]{1,0:T(8,128)S(1)} %get-tuple-element.23.mask, f32[48,640]{1,0:T(8,128)S(1)} %collective-permute-done.above.below, ...), custom_call_target="tpu_custom_call" | custom-call | flops 2949120000 | bytes 25165824 | tf_op jit(solution)/shard_map/windows/pallas_call | solution.py:545
  39.6 1.8 %collective-permute-start.5 = (bf16[336,640]{1,0:T(8,128)(2,1)S(1)}, bf16[336,640]{1,0:T(8,128)(2,1)S(1)}, u32[]{:S(2)}, u32[]{:S(2)}) collective-permute-start(bf16[336,640]{1,0:T(8,128)(2,1)S(1)} %collective-permute-done.4.two), channel_id=1, source_target_pairs={{0,16},{4,12},{8,24},{12,4},{16,0},{20,28},{24,8},{28,20},{1,17},{... | collective-permute-start | bytes 1290248 | tf_op jit(solution)/shard_map/ppermute | solution.py:34
  41.4 2.2 %next.1.total = f32[800,640]{1,0:T(8,128)S(1)} custom-call(bf16[6,4,880,128]{3,2,1,0:T(8,128)(2,1)S(1)} %get-tuple-element.30.src, bf16[8,800,208]{2,1,0:T(8,128)(2,1)S(1)} %get-tuple-element.31.packs, bf16[384,640]{1,0:T(8,128)(2,1)S(1)} %collective-permute-done.9.one, bf16[336,640]{1,0:T(8,128)(2,1)S(1)} %collective-permute-done.4.two, ...), custom_call_target="tpu_custom_call" | custom-call | flops 1474560000 | bytes 4194304 | tf_op jit(solution)/shard_map/next/pallas_call | solution.py:571
  43.9 3.9 %collective-permute-done.5.piece = bf16[336,640]{1,0:T(8,128)(2,1)S(1)} collective-permute-done((bf16[336,640]{1,0:T(8,128)(2,1)S(1)}, bf16[336,640]{1,0:T(8,128)(2,1)S(1)}, u32[]{:S(2)}, u32[]{:S(2)}) %collective-permute-start.5) | collective-permute-done | bytes 430112 | tf_op jit(solution)/shard_map/ppermute | solution.py:34
  47.8 0.8 %piece.5.total = f32[800,640]{1,0:T(8,128)S(1)} custom-call(bf16[6,4,880,128]{3,2,1,0:T(8,128)(2,1)S(1)} %get-tuple-element.30.src, bf16[8,800,208]{2,1,0:T(8,128)(2,1)S(1)} %get-tuple-element.31.packs, bf16[384,640]{1,0:T(8,128)(2,1)S(1)} %collective-permute-done.10.piece, f32[800,640]{1,0:T(8,128)S(1)} %next.1.total), custom_call_target="tpu_custom_call" | custom-call | flops 737280000 | bytes 4194304 | tf_op jit(solution)/shard_map/piece/pallas_call | solution.py:583
  48.6 0.8 %piece.6.total = f32[800,640]{1,0:T(8,128)S(1)} custom-call(bf16[6,4,880,128]{3,2,1,0:T(8,128)(2,1)S(1)} %get-tuple-element.30.src, bf16[8,800,208]{2,1,0:T(8,128)(2,1)S(1)} %get-tuple-element.31.packs, bf16[384,640]{1,0:T(8,128)(2,1)S(1)} %collective-permute-done.13.piece, f32[800,640]{1,0:T(8,128)S(1)} %piece.5.total), custom_call_target="tpu_custom_call" | custom-call | flops 737280000 | bytes 4194304 | tf_op jit(solution)/shard_map/piece/pallas_call | solution.py:583
  49.4 1.4 %piece.7.total = f32[800,640]{1,0:T(8,128)S(1)} custom-call(bf16[6,4,880,128]{3,2,1,0:T(8,128)(2,1)S(1)} %get-tuple-element.30.src, bf16[8,800,208]{2,1,0:T(8,128)(2,1)S(1)} %get-tuple-element.31.packs, bf16[720,640]{1,0:T(8,128)(2,1)S(1)} %collective-permute-done.7.piece, f32[800,640]{1,0:T(8,128)S(1)} %piece.6.total), custom_call_target="tpu_custom_call" | custom-call | flops 737280000 | bytes 4194304 | tf_op jit(solution)/shard_map/piece/pallas_call | solution.py:583
  50.8 0.8 %piece.8.total = f32[800,640]{1,0:T(8,128)S(1)} custom-call(bf16[6,4,880,128]{3,2,1,0:T(8,128)(2,1)S(1)} %get-tuple-element.30.src, bf16[8,800,208]{2,1,0:T(8,128)(2,1)S(1)} %get-tuple-element.31.packs, bf16[336,640]{1,0:T(8,128)(2,1)S(1)} %collective-permute-done.5.piece, f32[800,640]{1,0:T(8,128)S(1)} %piece.7.total), custom_call_target="tpu_custom_call" | custom-call | flops 737280000 | bytes 4194304 | tf_op jit(solution)/shard_map/piece/pallas_call | solution.py:583
  51.5 1.2 %piece.9.total = f32[800,640]{1,0:T(8,128)S(1)} custom-call(bf16[6,4,880,128]{3,2,1,0:T(8,128)(2,1)S(1)} %get-tuple-element.30.src, bf16[8,800,208]{2,1,0:T(8,128)(2,1)S(1)} %get-tuple-element.31.packs, bf16[720,640]{1,0:T(8,128)(2,1)S(1)} %collective-permute-done.8.piece, f32[800,640]{1,0:T(8,128)S(1)} %piece.8.total), custom_call_target="tpu_custom_call" | custom-call | flops 737280000 | bytes 4194304 | tf_op jit(solution)/shard_map/piece/pallas_call | solution.py:583
  52.8 1.5 %last.1 = bf16[800,640]{1,0:T(8,128)(2,1)} custom-call(bf16[6,4,880,128]{3,2,1,0:T(8,128)(2,1)S(1)} %get-tuple-element.30.src, bf16[8,800,208]{2,1,0:T(8,128)(2,1)S(1)} %get-tuple-element.31.packs, bf16[336,640]{1,0:T(8,128)(2,1)S(1)} %collective-permute-done.6.piece, f32[800,640]{1,0:T(8,128)S(1)} %piece.9.total), custom_call_target="tpu_custom_call" | custom-call | flops 368640000 | bytes 4194304 | tf_op jit(solution)/shard_map/last/pallas_call | solution.py:600
  (36 shorter events, 0.8 us)
Async XLA Ops:
  0.0 1.2 %copy-start.1 = (bf16[1,20,40,640]{3,2,1,0:T(8,128)(2,1)S(1)}, bf16[1,20,40,640]{3,2,1,0:T(8,128)(2,1)}, u32[]{:S(2)}) copy-start(bf16[1,20,40,640]{3,2,1,0:T(8,128)(2,1)} %param.7) | copy-start | bytes 3072004
  1.2 3.2 %copy-start.2 = (bf16[1,20,40,640]{3,2,1,0:T(8,128)(2,1)S(1)}, bf16[1,20,40,640]{3,2,1,0:T(8,128)(2,1)}, u32[]{:S(2)}) copy-start(bf16[1,20,40,640]{3,2,1,0:T(8,128)(2,1)} %param.7) | copy-start | bytes 3072004
  2.4 2.0 %collective-permute-start = (f32[48,640]{1,0:T(8,128)S(1)}, f32[48,640]{1,0:T(8,128)S(1)}, u32[]{:S(2)}, u32[]{:S(2)}) collective-permute-start(f32[48,640]{1,0:T(8,128)S(1)} %broadcast_select_fusion), channel_id=1, source_target_pairs={{0,4},{4,0},{1,5},{5,1},{2,6},{6,2},{3,7},{7,3},{8,12},{12,8},{9,1... | collective-permute-start | bytes 368648 | tf_op jit(solution)/shard_map/ppermute | solution.py:26
  4.3 27.2 %copy-start.4 = (f32[640]{0:T(1024)S(1)}, f32[640]{0:T(1024)}, u32[]{:S(2)}) copy-start(f32[640]{0:T(1024)} %param.10) | copy-start | bytes 7684
  4.4 27.2 %copy-start.5 = (f32[640]{0:T(1024)S(1)}, f32[640]{0:T(1024)}, u32[]{:S(2)}) copy-start(f32[640]{0:T(1024)} %param.13) | copy-start | bytes 7684
  4.4 27.2 %copy-start.6 = (f32[640]{0:T(1024)S(1)}, f32[640]{0:T(1024)}, u32[]{:S(2)}) copy-start(f32[640]{0:T(1024)} %param.9) | copy-start | bytes 7684
  4.4 28.8 %copy-start = (bf16[9,160,640]{2,1,0:T(8,128)(2,1)S(1)}, bf16[9,160,640]{2,1,0:T(8,128)(2,1)}, u32[]{:S(2)}) copy-start(bf16[9,160,640]{2,1,0:T(8,128)(2,1)} %weight.5) | copy-start | bytes 5529604
  4.4 28.8 %copy-start.3 = (f32[9,640]{1,0:T(8,128)S(1)}, f32[9,640]{1,0:T(8,128)}, u32[]{:S(2)}) copy-start(f32[9,640]{1,0:T(8,128)} %mask_weight.1) | copy-start | bytes 69124
  4.6 34.9 %collective-permute-start.7 = (bf16[720,640]{1,0:T(8,128)(2,1)S(1)}, bf16[720,640]{1,0:T(8,128)(2,1)S(1)}, u32[]{:S(2)}, u32[]{:S(2)}) collective-permute-start(bf16[720,640]{1,0:T(8,128)(2,1)S(1)} %cut.3), channel_id=1, source_target_pairs={{0,8},{4,20},{8,0},{12,28},{16,24},{20,4},{24,16},{28,12},{1,9},{5... | collective-permute-start | bytes 2764808 | tf_op jit(solution)/shard_map/ppermute | solution.py:34
  8.5 15.3 %collective-permute-start.9 = (bf16[384,640]{1,0:T(8,128)(2,1)S(1)}, bf16[384,640]{1,0:T(8,128)(2,1)S(1)}, u32[]{:S(2)}, u32[]{:S(2)}) collective-permute-start(bf16[384,640]{1,0:T(8,128)(2,1)S(1)} %get-tuple-element.37), channel_id=1, source_target_pairs={{0,8},{4,20},{8,0},{12,28},{16,24},{20,4},{24,16},{28,12},{1,9},{5... | collective-permute-start | bytes 1474568 | tf_op jit(solution)/shard_map/ppermute | solution.py:34
  8.7 19.7 %collective-permute-start.4 = (bf16[336,640]{1,0:T(8,128)(2,1)S(1)}, bf16[336,640]{1,0:T(8,128)(2,1)S(1)}, u32[]{:S(2)}, u32[]{:S(2)}) collective-permute-start(bf16[336,640]{1,0:T(8,128)(2,1)S(1)} %get-tuple-element.32), channel_id=1, source_target_pairs={{0,8},{4,20},{8,0},{12,28},{16,24},{20,4},{24,16},{28,12},{1,9},{5... | collective-permute-start | bytes 1290248 | tf_op jit(solution)/shard_map/ppermute | solution.py:34
  10.6 4.4 %collective-permute-start.1 = (bf16[48,768]{1,0:T(8,128)(2,1)S(1)}, bf16[48,768]{1,0:T(8,128)(2,1)S(1)}, u32[]{:S(2)}, u32[]{:S(2)}) collective-permute-start(bf16[48,768]{1,0:T(8,128)(2,1)S(1)} %get-tuple-element.27), channel_id=1, source_target_pairs={{0,1},{1,0},{2,3},{3,2},{4,5},{5,4},{6,7},{7,6},{8,9},{9,8},{10,11... | collective-permute-start | bytes 221192 | tf_op jit(solution)/shard_map/ppermute | solution.py:26
  23.8 17.6 %collective-permute-start.11 = (bf16[384,640]{1,0:T(8,128)(2,1)S(1)}, bf16[384,640]{1,0:T(8,128)(2,1)S(1)}, u32[]{:S(2)}, u32[]{:S(2)}) collective-permute-start(bf16[384,640]{1,0:T(8,128)(2,1)S(1)} %collective-permute-done.9.one), channel_id=1, source_target_pairs={{0,4},{4,0},{1,5},{5,1},{2,6},{6,2},{3,7},{7,3},{8,12},{12,8},{9,1... | collective-permute-start | bytes 1474568 | tf_op jit(solution)/shard_map/ppermute | solution.py:26
  23.8 7.8 %collective-permute-start.2 = (bf16[48,768]{1,0:T(8,128)(2,1)S(1)}, bf16[48,768]{1,0:T(8,128)(2,1)S(1)}, u32[]{:S(2)}, u32[]{:S(2)}) collective-permute-start(bf16[48,768]{1,0:T(8,128)(2,1)S(1)} %get-tuple-element.28), channel_id=1, source_target_pairs={{1,2},{2,1},{5,6},{6,5},{9,10},{10,9},{13,14},{14,13},{17,18},{18,... | collective-permute-start | bytes 221192 | tf_op jit(solution)/shard_map/ppermute | solution.py:527
  28.4 13.0 %collective-permute-start.12 = (bf16[336,640]{1,0:T(8,128)(2,1)S(1)}, bf16[336,640]{1,0:T(8,128)(2,1)S(1)}, u32[]{:S(2)}, u32[]{:S(2)}) collective-permute-start(bf16[336,640]{1,0:T(8,128)(2,1)S(1)} %collective-permute-done.4.two), channel_id=1, source_target_pairs={{0,4},{4,0},{1,5},{5,1},{2,6},{6,2},{3,7},{7,3},{8,12},{12,8},{9,1... | collective-permute-start | bytes 1290248 | tf_op jit(solution)/shard_map/ppermute | solution.py:26
  28.4 4.8 %collective-permute-start.3 = (f32[8,128]{1,0:T(8,128)S(1)}, f32[8,128]{1,0:T(8,128)S(1)}, u32[]{:S(2)}, u32[]{:S(2)}) collective-permute-start(f32[8,128]{1,0:T(8,128)S(1)} %message_two.1.own), channel_id=1, source_target_pairs={{0,2},{1,3},{2,0},{3,1},{4,6},{5,7},{6,4},{7,5},{8,10},{9,11},{10,... | collective-permute-start | bytes 12296 | tf_op jit(solution)/shard_map/ppermute | solution.py:26
  31.6 12.0 %collective-permute-start.10 = (bf16[384,640]{1,0:T(8,128)(2,1)S(1)}, bf16[384,640]{1,0:T(8,128)(2,1)S(1)}, u32[]{:S(2)}, u32[]{:S(2)}) collective-permute-start(bf16[384,640]{1,0:T(8,128)(2,1)S(1)} %collective-permute-done.9.one), channel_id=1, source_target_pairs={{0,16},{4,12},{8,24},{12,4},{16,0},{20,28},{24,8},{28,20},{1,17},{... | collective-permute-start | bytes 1474568 | tf_op jit(solution)/shard_map/ppermute | solution.py:34
  39.5 12.0 %collective-permute-start.8 = (bf16[720,640]{1,0:T(8,128)(2,1)S(1)}, bf16[720,640]{1,0:T(8,128)(2,1)S(1)}, u32[]{:S(2)}, u32[]{:S(2)}) collective-permute-start(bf16[720,640]{1,0:T(8,128)(2,1)S(1)} %collective-permute-done.7.piece), channel_id=1, source_target_pairs={{0,4},{4,0},{1,5},{5,1},{2,6},{6,2},{3,7},{7,3},{8,12},{12,8},{9,1... | collective-permute-start | bytes 2764808 | tf_op jit(solution)/shard_map/ppermute | solution.py:26
  39.6 8.2 %collective-permute-start.5 = (bf16[336,640]{1,0:T(8,128)(2,1)S(1)}, bf16[336,640]{1,0:T(8,128)(2,1)S(1)}, u32[]{:S(2)}, u32[]{:S(2)}) collective-permute-start(bf16[336,640]{1,0:T(8,128)(2,1)S(1)} %collective-permute-done.4.two), channel_id=1, source_target_pairs={{0,16},{4,12},{8,24},{12,4},{16,0},{20,28},{24,8},{28,20},{1,17},{... | collective-permute-start | bytes 1290248 | tf_op jit(solution)/shard_map/ppermute | solution.py:34
  43.7 4.9 %collective-permute-start.13 = (bf16[384,640]{1,0:T(8,128)(2,1)S(1)}, bf16[384,640]{1,0:T(8,128)(2,1)S(1)}, u32[]{:S(2)}, u32[]{:S(2)}) collective-permute-start(bf16[384,640]{1,0:T(8,128)(2,1)S(1)} %collective-permute-done.10.piece), channel_id=1, source_target_pairs={{0,4},{4,0},{1,5},{5,1},{2,6},{6,2},{3,7},{7,3},{8,12},{12,8},{9,1... | collective-permute-start | bytes 1474568 | tf_op jit(solution)/shard_map/ppermute | solution.py:26
  47.8 4.9 %collective-permute-start.6 = (bf16[336,640]{1,0:T(8,128)(2,1)S(1)}, bf16[336,640]{1,0:T(8,128)(2,1)S(1)}, u32[]{:S(2)}, u32[]{:S(2)}) collective-permute-start(bf16[336,640]{1,0:T(8,128)(2,1)S(1)} %collective-permute-done.5.piece), channel_id=1, source_target_pairs={{0,4},{4,0},{1,5},{5,1},{2,6},{6,2},{3,7},{7,3},{8,12},{12,8},{9,1... | collective-permute-start | bytes 1290248 | tf_op jit(solution)/shard_map/ppermute | solution.py:26
